TPU v7x, 512 devices: a whole 4x4x16 slice. The times are simulated.
512 devices in a mesh: blk: 128 (over z, x, core), grp: 4 (over y).
Axes of the slice: x: 4, y: 4, z: 16, core: 2. Of those that a mesh axis runs over, the one named last changes fastest.
Arguments:
- checkpoint: bfloat16 [131072, 320], P(('blk', 'grp')), may hold values from -4 to 4
- adjoint_rhs: bfloat16 [131072, 320], P(('blk', 'grp')), may hold values from -6 to 6
- new_position: int32 [131072], P(('blk', 'grp')), may hold values from 0 to 131071, as said below
- old_position: int32 [131072], P(('blk', 'grp')), may hold values from 0 to 131071, as said below
- left_matrix: bfloat16 [320, 320], replicated, may hold values from -0.3125 to 0.3125
- right_matrix: bfloat16 [320, 320], replicated, may hold values from -0.3125 to 0.3125
- face_block: int32 [6, 131072], P(None, ('blk', 'grp')), may hold values from -1 to 131071, as said below
- face_weight: float32 [6, 131072], P(None, ('blk', 'grp')), may hold values from 0.3 to 0.9
- donor_block: int32 [2, 131072], P(None, ('blk', 'grp')), may hold values from 0 to 131071, as said below
- donor_weight: float32 [2, 131072], P(None, ('blk', 'grp')), may hold values from 0.2 to 0.7
Outputs:
- adjoint: float32 [131072, 320], P(('blk', 'grp'))
Inputs may be any that keep to these rules, and one draw needn't show every extreme that they name: `new_position`: A permutation of the block indices that keeps each block's index along grp; the blocks of one device go to 64 devices along blk, exactly 4 blocks to each of them. `old_position`: the inverse permutation of new_position. `face_block`: each entry is -1 or a block of the same grp index whose place in that group's order of blocks (blk index times 256 plus the local index) lies within 256 places of the block's own, taken cyclically. `donor_block`: each donor lies on the device of the same blk index and another grp index, among the first 128 blocks of that device in the new order.
All inputs are finite; a program needn't handle non-finite values.
Results may differ from a plain program's by a relative error of at most 0.0014.
Values may be sent and summed in bfloat16 or wider, within the bound.
A program may use at most 64 MiB of HBM per device.

v0:
```python
import jax
import jax.numpy as jnp
from jax import lax
from jax.sharding import PartitionSpec as P


def passed_along(block, axis, distance):
    devices = range(lax.axis_size(axis))
    route = [((i - distance) % len(devices), i) for i in devices]
    return lax.ppermute(block, axis, route)


def coefficients(state):
    values = state.astype(jnp.float32)
    left_gain = 0.5 * jnp.tanh(values)
    right_gain = 0.4 * jnp.tanh(1.5 * values - 0.5)
    dual_diag = 2.0 + values * values
    return (left_gain, right_gain, dual_diag)


def transposed_apply(
    adjoint, left_gain, right_gain, left_matrix, right_matrix, left_trans, right_trans
):
    rounded = adjoint.astype(jnp.bfloat16)
    first_proj = jnp.dot(rounded, left_matrix, preferred_element_type=jnp.float32)
    second_proj = jnp.dot(rounded, right_trans, preferred_element_type=jnp.float32)
    first_mid = (first_proj * left_gain).astype(jnp.bfloat16)
    second_mid = (second_proj * right_gain).astype(jnp.bfloat16)
    return jnp.dot(first_mid, right_matrix, preferred_element_type=jnp.float32) + jnp.dot(
        second_mid, left_trans, preferred_element_type=jnp.float32
    )


def face_sum(block_pool, face_index, face_valid, face_weight):
    row_count = face_index.shape[1]
    total_face = jnp.zeros((row_count, block_pool.shape[1]), jnp.float32)
    for face_id in range(face_index.shape[0]):
        fetched = jnp.take(block_pool, face_index[face_id], axis=0).reshape(row_count, 5, 4, 4, 4)
        cell_axis = 2 + face_id // 2
        from_cell = 3 if face_id % 2 == 0 else 0
        face_slab = lax.slice_in_dim(fetched, from_cell, from_cell + 1, axis=cell_axis)
        scale_face = jnp.where(face_valid[face_id], face_weight[face_id], 0.0)
        face_slab = face_slab * scale_face.reshape(row_count, 1, 1, 1, 1)
        pad_shape = list(face_slab.shape)
        pad_shape[cell_axis] = 3
        padding = jnp.zeros(pad_shape, jnp.float32)
        if face_id % 2 == 0:
            placed = jnp.concatenate([face_slab, padding], axis=cell_axis)
        else:
            placed = jnp.concatenate([padding, face_slab], axis=cell_axis)
        total_face = total_face + placed.reshape(row_count, block_pool.shape[1])
    return total_face


def fringe_sum(block_pool, donor_index, donor_weight):
    total_fringe = jnp.zeros((donor_index.shape[1], block_pool.shape[1]), jnp.float32)
    for donor_id in range(donor_index.shape[0]):
        fetched = jnp.take(block_pool, donor_index[donor_id], axis=0)
        total_fringe = total_fringe + donor_weight[donor_id][:, None] * fetched
    return total_fringe


def body(
    checkpoint,
    adjoint_rhs,
    new_position,
    old_position,
    left_matrix,
    right_matrix,
    face_block,
    face_weight,
    donor_block,
    donor_weight,
):
    blk_count = lax.axis_size("blk")
    grp_count = lax.axis_size("grp")
    per_device = checkpoint.shape[0]
    capacity = max(2, 2 * per_device // blk_count)
    my_blk = lax.axis_index("blk")
    left_trans = left_matrix.T
    right_trans = right_matrix.T
    target = new_position // per_device // grp_count
    positions = jnp.arange(per_device, dtype=jnp.int32)
    send_rank = jnp.sum(
        (target[:, None] == target[None, :]) & (positions[None, :] < positions[:, None]), axis=1
    )
    send_slot = target * capacity + send_rank
    anchor = old_position // per_device // grp_count
    anchor_local = old_position % per_device
    recv_rank = jnp.sum(
        (anchor[:, None] == anchor[None, :]) & (anchor_local[None, :] < anchor_local[:, None]),
        axis=1,
    )
    recv_slot = anchor * capacity + recv_rank
    face_valid = face_block >= 0
    face_blk = face_block // per_device // grp_count
    face_place = (face_blk - my_blk + 1) % blk_count * per_device + face_block % per_device
    face_local = jnp.where(face_valid, face_place, 0)
    donor_grp = donor_block // per_device % grp_count
    donor_within = donor_block % per_device

    def pack_rows(values, slot_ids):
        buffer = (
            jnp.zeros((blk_count * capacity, values.shape[1]), values.dtype)
            .at[slot_ids]
            .set(values)
        )
        return buffer.reshape(blk_count, capacity, values.shape[1])

    def unpack_rows(received, slot_ids):
        return received.reshape(blk_count * capacity, received.shape[2])[slot_ids]

    got_state, got_rhs = (
        lax.all_to_all(
            pack_rows(checkpoint, send_slot), "blk", split_axis=0, concat_axis=0, tiled=True
        ),
        lax.all_to_all(
            pack_rows(adjoint_rhs, send_slot), "blk", split_axis=0, concat_axis=0, tiled=True
        ),
    )
    state_new = unpack_rows(got_state, recv_slot)
    rhs_float = unpack_rows(got_rhs, recv_slot).astype(jnp.float32)
    left_gain, right_gain, dual_diag = coefficients(state_new)
    result = rhs_float / dual_diag
    for sweep_step in range(2):
        applied = transposed_apply(
            result, left_gain, right_gain, left_matrix, right_matrix, left_trans, right_trans
        )
        below_adj = passed_along(result.astype(jnp.bfloat16), "blk", 1).astype(result.dtype)
        above_adj = passed_along(result.astype(jnp.bfloat16), "blk", -1).astype(result.dtype)
        block_pool = jnp.concatenate([below_adj, result, above_adj], axis=0)
        face_term = face_sum(block_pool, face_local, face_valid, face_weight)
        group_pool = lax.all_gather(result, "grp", axis=0, tiled=True)
        donor_local = donor_grp * per_device + donor_within
        fringe_term = fringe_sum(group_pool, donor_local, donor_weight)
        face_term, fringe_term = (face_term, fringe_term)
        result = (rhs_float - applied - face_term - fringe_term) / dual_diag
    return result


def solution(mesh):
    in_specs = (
        P(("blk", "grp"), None),
        P(("blk", "grp"), None),
        P(("blk", "grp")),
        P(("blk", "grp")),
        P(),
        P(),
        P(None, ("blk", "grp")),
        P(None, ("blk", "grp")),
        P(None, ("blk", "grp")),
        P(None, ("blk", "grp")),
    )
    out_specs = P(("blk", "grp"), None)
    return jax.shard_map(body, mesh=mesh, in_specs=in_specs, out_specs=out_specs, check_vma=False)
```

profile of v0, /device:TPU:1, one launch (start us, length us, event | category | flops | bytes accessed | tf_op | source)
XLA Modules:
  0.0 188.1 jit_solution(17737311999590870322)
XLA Ops:
  8.2 1.1 copy.83
  9.3 1.6 scatter_custom_fusion.1
  10.9 0.9 reshape.182
  11.7 20.5 %all-to-all-start.1 = ((bf16[128,4,320]{2,1,0:T(4,128)(2,1)}), bf16[128,4,320]{2,1,0:T(4,128)(2,1)S(1)}, u32[]{:S(2)}, u32[]{:S(2)}) async-start(bf16[128,4,320]{2,1,0:T(4,128)(2,1)} %reshape.182), calls=%async_computation.1 | async-start | bytes 786432 | tf_op jit(solution)/shard_map/all_to_all | solution.py:114
  32.7 1.6 scatter_custom_fusion
  34.3 0.9 reshape.180
  35.7 21.9 %all-to-all-done.1 = bf16[128,4,320]{2,1,0:T(4,128)(2,1)S(1)} async-done(((bf16[128,4,320]{2,1,0:T(4,128)(2,1)}), bf16[128,4,320]{2,1,0:T(4,128)(2,1)S(1)}, u32[]{:S(2)}, u32[]{:S(2)}) %all-to-all-start.1) | async-done | bytes 327712 | tf_op jit(solution)/shard_map/all_to_all | solution.py:114
  57.6 8.9 %all-to-all-start = ((bf16[128,4,320]{2,1,0:T(4,128)(2,1)}), bf16[128,4,320]{2,1,0:T(4,128)(2,1)S(1)}, u32[]{:S(2)}, u32[]{:S(2)}) async-start(bf16[128,4,320]{2,1,0:T(4,128)(2,1)} %reshape.180), calls=%async_computation | async-start | bytes 786432 | tf_op jit(solution)/shard_map/all_to_all | solution.py:117
  67.0 1.2 gather_fusion.1
  68.3 23.6 %all-to-all-done = bf16[128,4,320]{2,1,0:T(4,128)(2,1)S(1)} async-done(((bf16[128,4,320]{2,1,0:T(4,128)(2,1)}), bf16[128,4,320]{2,1,0:T(4,128)(2,1)S(1)}, u32[]{:S(2)}, u32[]{:S(2)}) %all-to-all-start) | async-done | bytes 327712 | tf_op jit(solution)/shard_map/all_to_all | solution.py:117
  92.2 1.2 gather_fusion
  93.5 0.8 convert_divide_fusion
  94.3 4.4 %collective-permute-start = (bf16[256,320]{0,1:T(8,128)(2,1)S(1)}, bf16[256,320]{0,1:T(8,128)(2,1)S(1)}, u32[]{:S(2)}, u32[]{:S(2)}) collective-permute-start(bf16[256,320]{0,1:T(8,128)(2,1)S(1)} %get-tuple-element.8), channel_id=1, source_target_pairs={{508,0},{0,4},{4,8},{8,12},{12,16},{16,20},{20,24},{24,28},{28,32}... | collective-permute-start | bytes 491528 | tf_op jit(solution)/shard_map/ppermute | solution.py:10
  98.7 1.9 %collective-permute-start.1 = (bf16[256,320]{0,1:T(8,128)(2,1)S(1)}, bf16[256,320]{0,1:T(8,128)(2,1)S(1)}, u32[]{:S(2)}, u32[]{:S(2)}) collective-permute-start(bf16[256,320]{0,1:T(8,128)(2,1)S(1)} %get-tuple-element.8), channel_id=1, source_target_pairs={{4,0},{8,4},{12,8},{16,12},{20,16},{24,20},{28,24},{32,28},{36,32}... | collective-permute-start | bytes 491528 | tf_op jit(solution)/shard_map/ppermute | solution.py:10
  100.9 1.4 fusion.13
  102.3 3.0 %collective-permute-done.1 = bf16[256,320]{0,1:T(8,128)(2,1)S(1)} collective-permute-done((bf16[256,320]{0,1:T(8,128)(2,1)S(1)}, bf16[256,320]{0,1:T(8,128)(2,1)S(1)}, u32[]{:S(2)}, u32[]{:S(2)}) %collective-permute-start.1) | collective-permute-done | bytes 163872 | tf_op jit(solution)/shard_map/ppermute | solution.py:10
  105.8 1.0 gather_fusion.2
  107.2 1.0 gather_fusion.3
  108.6 1.0 gather_fusion.4
  109.8 0.8 reshape.186
  110.6 1.0 gather_fusion.5
  111.9 0.8 reshape.187
  112.7 1.0 gather_fusion.6
  114.0 0.8 reshape.188
  114.8 1.0 gather_fusion.7
  116.3 1.0 slice_multiply_fusion.8
  117.2 1.1 slice_multiply_fusion.6
  118.7 9.3 %all-gather.3.cloned.1.call-done = f32[1024,320]{0,1:T(8,128)} async-done(((f32[256,320]{0,1:T(8,128)}), f32[1024,320]{0,1:T(8,128)}) %all-gather.3.cloned.1.call-update) | async-done | bytes 1310736 | tf_op jit(solution)/shard_map/all_gather | solution.py:133
  128.0 1.8 copy.97
  129.8 1.0 gather_fusion.9
  130.9 1.0 gather_fusion.8
  132.1 2.5 %fusion.66 = (bf16[256,320]{0,1:T(8,128)(2,1)S(1)}, f32[256,320]{0,1:T(8,128)}) fusion(bf16[256,320]{0,1:T(8,128)(2,1)S(1)} %copy.84, f32[256,320]{0,1:T(8,128)S(1)} %copy.100, pred[256]{0:T(512)(128)(4,1)S(1)} %get-tuple-element.35, f32[256]{0:T(256)S(1)} %bitcast.84, f32[256,320]{0,1:T(8,128)S(1)} %copy.98, pred[256]{0:T(512)(128)(4,1)S(1)} %get-tuple-element.36, ...), kind=kOutput, calls=%fused_computation.198 | convolution fusion | flops 107069440 | bytes 2542080 | tf_op jit(solution)/shard_map/dot_general | solution.py:29
  134.6 4.8 %collective-permute-start.2 = (bf16[256,320]{0,1:T(8,128)(2,1)S(1)}, bf16[256,320]{0,1:T(8,128)(2,1)S(1)}, u32[]{:S(2)}, u32[]{:S(2)}) collective-permute-start(bf16[256,320]{0,1:T(8,128)(2,1)S(1)} %get-tuple-element.27), channel_id=1, source_target_pairs={{508,0},{0,4},{4,8},{8,12},{12,16},{16,20},{20,24},{24,28},{28,32}... | collective-permute-start | bytes 491528 | tf_op jit(solution)/shard_map/ppermute | solution.py:10
  139.5 2.1 %collective-permute-start.3 = (bf16[256,320]{0,1:T(8,128)(2,1)S(1)}, bf16[256,320]{0,1:T(8,128)(2,1)S(1)}, u32[]{:S(2)}, u32[]{:S(2)}) collective-permute-start(bf16[256,320]{0,1:T(8,128)(2,1)S(1)} %get-tuple-element.27), channel_id=1, source_target_pairs={{4,0},{8,4},{12,8},{16,12},{20,16},{24,20},{28,24},{32,28},{36,32}... | collective-permute-start | bytes 491528 | tf_op jit(solution)/shard_map/ppermute | solution.py:10
  141.6 1.4 fusion.12
  143.1 3.0 %collective-permute-done.3 = bf16[256,320]{0,1:T(8,128)(2,1)S(1)} collective-permute-done((bf16[256,320]{0,1:T(8,128)(2,1)S(1)}, bf16[256,320]{0,1:T(8,128)(2,1)S(1)}, u32[]{:S(2)}, u32[]{:S(2)}) %collective-permute-start.3) | collective-permute-done | bytes 163872 | tf_op jit(solution)/shard_map/ppermute | solution.py:10
  146.6 1.9 gather_fusion.14
  148.4 1.1 gather_fusion.13
  149.6 1.1 gather_fusion.12
  150.7 1.1 gather_fusion.11
  151.8 1.1 gather_fusion.10
  152.9 1.1 gather_fusion.15
  154.1 1.1 broadcast_select_fusion.1
  159.2 15.4 %all-gather.5.cloned.1.call-done = f32[1024,320]{0,1:T(8,128)} async-done(((f32[256,320]{0,1:T(8,128)}), f32[1024,320]{0,1:T(8,128)}) %all-gather.5.cloned.1.call-update) | async-done | bytes 1310736 | tf_op jit(solution)/shard_map/all_gather | solution.py:133
  174.6 1.8 copy.113
  176.4 1.1 gather_fusion.16
  177.5 1.1 gather_fusion.17
  179.9 1.3 fusion.7
  (215 shorter events, 11.6 us)
Async XLA Ops:
  6.5 94.3 %copy-start = (bf16[320,320]{1,0:T(8,128)(2,1)S(1)}, bf16[320,320]{1,0:T(8,128)(2,1)}, u32[]{:S(2)}) copy-start(bf16[320,320]{1,0:T(8,128)(2,1)} %param.19) | copy-start | bytes 614404
  6.5 25.7 %copy-start.47 = (s32[256]{0:T(256)S(1)}, s32[256]{0:T(256)}, u32[]{:S(2)}) copy-start(s32[256]{0:T(256)} %param.17) | copy-start | bytes 3076
  6.5 26.0 %copy-start.11 = (bf16[256,320]{0,1:T(8,128)(2,1)S(1)}, bf16[256,320]{0,1:T(8,128)(2,1)}, u32[]{:S(2)}) copy-start(bf16[256,320]{0,1:T(8,128)(2,1)} %param.15) | copy-start | bytes 491524
  11.7 23.5 %copy-start.12 = (s32[6,256]{1,0:T(8,128)S(1)}, s32[6,256]{1,0:T(8,128)}, u32[]{:S(2)}) copy-start(s32[6,256]{1,0:T(8,128)} %param.20) | copy-start | bytes 18436
  11.7 23.8 %copy-start.34 = (s32[2,256]{1,0:T(2,128)S(1)}, s32[2,256]{1,0:T(2,128)}, u32[]{:S(2)}) copy-start(s32[2,256]{1,0:T(2,128)} %param.22) | copy-start | bytes 6148
  11.7 45.9 %all-to-all-start.1 = ((bf16[128,4,320]{2,1,0:T(4,128)(2,1)}), bf16[128,4,320]{2,1,0:T(4,128)(2,1)S(1)}, u32[]{:S(2)}, u32[]{:S(2)}) async-start(bf16[128,4,320]{2,1,0:T(4,128)(2,1)} %reshape.182), calls=%async_computation.1 | async-start | bytes 786432 | tf_op jit(solution)/shard_map/all_to_all | solution.py:114
  32.5 34.2 %copy-start.35 = (f32[2,256]{1,0:T(2,128)S(1)}, f32[2,256]{1,0:T(2,128)}, u32[]{:S(2)}) copy-start(f32[2,256]{1,0:T(2,128)} %param.23) | copy-start | bytes 6148
  32.5 34.2 %copy-start.33 = (f32[6,256]{1,0:T(8,128)S(1)}, f32[6,256]{1,0:T(8,128)}, u32[]{:S(2)}) copy-start(f32[6,256]{1,0:T(8,128)} %param.21) | copy-start | bytes 18436
  35.3 70.5 %copy-start.27 = (s32[1024]{0:T(1024)}, s32[1024]{0:T(1024)S(1)}, u32[]{:S(2)}) copy-start(s32[1024]{0:T(1024)S(1)} %pad_clamp_fusion.7) | copy-start | bytes 12292
  35.3 71.8 %copy-start.28 = (s32[1024]{0:T(1024)}, s32[1024]{0:T(1024)S(1)}, u32[]{:S(2)}) copy-start(s32[1024]{0:T(1024)S(1)} %pad_clamp_fusion.6) | copy-start | bytes 12292
  35.4 73.2 %copy-start.29 = (s32[1024]{0:T(1024)}, s32[1024]{0:T(1024)S(1)}, u32[]{:S(2)}) copy-start(s32[1024]{0:T(1024)S(1)} %pad_clamp_fusion.5) | copy-start | bytes 12292
  35.4 75.2 %copy-start.31 = (s32[1024]{0:T(1024)}, s32[1024]{0:T(1024)S(1)}, u32[]{:S(2)}) copy-start(s32[1024]{0:T(1024)S(1)} %pad_clamp_fusion.4) | copy-start | bytes 12292
  35.4 77.3 %copy-start.32 = (s32[1024]{0:T(1024)}, s32[1024]{0:T(1024)S(1)}, u32[]{:S(2)}) copy-start(s32[1024]{0:T(1024)S(1)} %pad_clamp_fusion.3) | copy-start | bytes 12292
  35.5 79.3 %copy-start.30 = (s32[1024]{0:T(1024)}, s32[1024]{0:T(1024)S(1)}, u32[]{:S(2)}) copy-start(s32[1024]{0:T(1024)S(1)} %pad_clamp_fusion.2) | copy-start | bytes 12292
  35.6 94.2 %copy-start.25 = (s32[1024]{0:T(1024)}, s32[1024]{0:T(1024)S(1)}, u32[]{:S(2)}) copy-start(s32[1024]{0:T(1024)S(1)} %pad_clamp_fusion) | copy-start | bytes 12292
  35.6 95.3 %copy-start.26 = (s32[1024]{0:T(1024)}, s32[1024]{0:T(1024)S(1)}, u32[]{:S(2)}) copy-start(s32[1024]{0:T(1024)S(1)} %pad_clamp_fusion.1) | copy-start | bytes 12292
  35.6 71.2 %copy-start.36 = (pred[256]{0:T(512)(128)(4,1)}, pred[256]{0:T(512)(128)(4,1)S(1)}, u32[]{:S(2)}) copy-start(pred[256]{0:T(512)(128)(4,1)S(1)} %compare_and_fusion.7) | copy-start | bytes 772
  35.6 72.5 %copy-start.38 = (pred[256]{0:T(512)(128)(4,1)}, pred[256]{0:T(512)(128)(4,1)S(1)}, u32[]{:S(2)}) copy-start(pred[256]{0:T(512)(128)(4,1)S(1)} %compare_and_fusion.6) | copy-start | bytes 772
  35.7 73.9 %copy-start.42 = (pred[256]{0:T(512)(128)(4,1)}, pred[256]{0:T(512)(128)(4,1)S(1)}, u32[]{:S(2)}) copy-start(pred[256]{0:T(512)(128)(4,1)S(1)} %compare_and_fusion.5) | copy-start | bytes 772
  35.7 75.9 %copy-start.44 = (pred[256]{0:T(512)(128)(4,1)}, pred[256]{0:T(512)(128)(4,1)S(1)}, u32[]{:S(2)}) copy-start(pred[256]{0:T(512)(128)(4,1)S(1)} %compare_and_fusion.4) | copy-start | bytes 772
  57.6 34.3 %all-to-all-start = ((bf16[128,4,320]{2,1,0:T(4,128)(2,1)}), bf16[128,4,320]{2,1,0:T(4,128)(2,1)S(1)}, u32[]{:S(2)}, u32[]{:S(2)}) async-start(bf16[128,4,320]{2,1,0:T(4,128)(2,1)} %reshape.180), calls=%async_computation | async-start | bytes 786432 | tf_op jit(solution)/shard_map/all_to_all | solution.py:117
  66.6 61.4 %all-gather.3.cloned.1.call-start = ((), (), s32[]{:S(2)}) async-start(), calls=%async_computation.2 | async-start | bytes 1638400 | tf_op jit(solution)/shard_map/all_gather | solution.py:133
  66.6 47.1 %copy-start.46 = (pred[256]{0:T(512)(128)(4,1)}, pred[256]{0:T(512)(128)(4,1)S(1)}, u32[]{:S(2)}) copy-start(pred[256]{0:T(512)(128)(4,1)S(1)} %compare_and_fusion.3) | copy-start | bytes 772
  66.7 49.1 %copy-start.40 = (pred[256]{0:T(512)(128)(4,1)}, pred[256]{0:T(512)(128)(4,1)S(1)}, u32[]{:S(2)}) copy-start(pred[256]{0:T(512)(128)(4,1)S(1)} %compare_and_fusion.2) | copy-start | bytes 772
  66.7 65.4 %copy-start.52 = (pred[256]{0:T(512)(128)(4,1)}, pred[256]{0:T(512)(128)(4,1)S(1)}, u32[]{:S(2)}) copy-start(pred[256]{0:T(512)(128)(4,1)S(1)} %get-tuple-element.35) | copy-start | bytes 772
  66.7 65.4 %copy-start.54 = (pred[256]{0:T(512)(128)(4,1)}, pred[256]{0:T(512)(128)(4,1)S(1)}, u32[]{:S(2)}) copy-start(pred[256]{0:T(512)(128)(4,1)S(1)} %get-tuple-element.36) | copy-start | bytes 772
  66.7 65.4 %copy-start.48 = (f32[1,256]{1,0:T(1,128)}, f32[1,256]{1,0:T(1,128)S(1)}, u32[]{:S(2)}) copy-start(f32[1,256]{1,0:T(1,128)S(1)} %get-tuple-element.21) | copy-start | bytes 3076
  66.7 65.4 %copy-start.50 = (f32[1,256]{1,0:T(1,128)}, f32[1,256]{1,0:T(1,128)S(1)}, u32[]{:S(2)}) copy-start(f32[1,256]{1,0:T(1,128)S(1)} %get-tuple-element.22) | copy-start | bytes 3076
  66.8 49.4 %copy-start.17 = (f32[1,256]{1,0:T(1,128)}, f32[1,256]{1,0:T(1,128)S(1)}, u32[]{:S(2)}) copy-start(f32[1,256]{1,0:T(1,128)S(1)} %get-tuple-element.9) | copy-start | bytes 3076
  66.8 49.4 %copy-start.19 = (f32[1,256]{1,0:T(1,128)}, f32[1,256]{1,0:T(1,128)S(1)}, u32[]{:S(2)}) copy-start(f32[1,256]{1,0:T(1,128)S(1)} %get-tuple-element.13) | copy-start | bytes 3076
  66.8 49.4 %copy-start.21 = (f32[1,256]{1,0:T(1,128)}, f32[1,256]{1,0:T(1,128)S(1)}, u32[]{:S(2)}) copy-start(f32[1,256]{1,0:T(1,128)S(1)} %get-tuple-element.12) | copy-start | bytes 3076
  66.8 49.4 %copy-start.23 = (f32[1,256]{1,0:T(1,128)}, f32[1,256]{1,0:T(1,128)S(1)}, u32[]{:S(2)}) copy-start(f32[1,256]{1,0:T(1,128)S(1)} %get-tuple-element.11) | copy-start | bytes 3076
  66.8 50.4 %copy-start.13 = (f32[1,256]{1,0:T(1,128)}, f32[1,256]{1,0:T(1,128)S(1)}, u32[]{:S(2)}) copy-start(f32[1,256]{1,0:T(1,128)S(1)} %get-tuple-element.14) | copy-start | bytes 3076
  66.8 50.4 %copy-start.15 = (f32[1,256]{1,0:T(1,128)}, f32[1,256]{1,0:T(1,128)S(1)}, u32[]{:S(2)}) copy-start(f32[1,256]{1,0:T(1,128)S(1)} %get-tuple-element.10) | copy-start | bytes 3076
  93.3 7.6 %copy-start.6 = (bf16[320,320]{1,0:T(8,128)(2,1)S(1)}, bf16[320,320]{1,0:T(8,128)(2,1)}, u32[]{:S(2)}) copy-start(bf16[320,320]{1,0:T(8,128)(2,1)} %param.18) | copy-start | bytes 614404
  93.5 38.7 %copy-start.3 = (bf16[256,320]{0,1:T(8,128)(2,1)}, bf16[256,320]{0,1:T(8,128)(2,1)S(1)}, u32[]{:S(2)}) copy-start(bf16[256,320]{0,1:T(8,128)(2,1)S(1)} %copy.82) | copy-start | bytes 491524
  94.3 8.0 %collective-permute-start = (bf16[256,320]{0,1:T(8,128)(2,1)S(1)}, bf16[256,320]{0,1:T(8,128)(2,1)S(1)}, u32[]{:S(2)}, u32[]{:S(2)}) collective-permute-start(bf16[256,320]{0,1:T(8,128)(2,1)S(1)} %get-tuple-element.8), channel_id=1, source_target_pairs={{508,0},{0,4},{4,8},{8,12},{12,16},{16,20},{20,24},{24,28},{28,32}... | collective-permute-start | bytes 491528 | tf_op jit(solution)/shard_map/ppermute | solution.py:10
  98.7 6.6 %collective-permute-start.1 = (bf16[256,320]{0,1:T(8,128)(2,1)S(1)}, bf16[256,320]{0,1:T(8,128)(2,1)S(1)}, u32[]{:S(2)}, u32[]{:S(2)}) collective-permute-start(bf16[256,320]{0,1:T(8,128)(2,1)S(1)} %get-tuple-element.8), channel_id=1, source_target_pairs={{4,0},{8,4},{12,8},{16,12},{20,16},{24,20},{28,24},{32,28},{36,32}... | collective-permute-start | bytes 491528 | tf_op jit(solution)/shard_map/ppermute | solution.py:10
  100.6 4.7 %copy-start.1 = (f32[256,320]{0,1:T(8,128)S(1)}, f32[256,320]{0,1:T(8,128)}, u32[]{:S(2)}) copy-start(f32[256,320]{0,1:T(8,128)} %get-tuple-element.6) | copy-start | bytes 983044
  100.7 74.0 %all-gather.5.cloned.1.call-start = ((), (), s32[]{:S(2)}) async-start(), calls=%async_computation.3 | async-start | bytes 1638400 | tf_op jit(solution)/shard_map/all_gather | solution.py:133
  132.1 9.5 %copy-start.7 = (bf16[320,320]{1,0:T(8,128)(2,1)S(1)}, bf16[320,320]{1,0:T(8,128)(2,1)}, u32[]{:S(2)}) copy-start(bf16[320,320]{1,0:T(8,128)(2,1)} %param.18) | copy-start | bytes 614404
  134.6 11.5 %copy-start.9 = (bf16[256,320]{0,1:T(8,128)(2,1)}, bf16[256,320]{0,1:T(8,128)(2,1)S(1)}, u32[]{:S(2)}) copy-start(bf16[256,320]{0,1:T(8,128)(2,1)S(1)} %get-tuple-element.27) | copy-start | bytes 491524
  134.6 8.4 %collective-permute-start.2 = (bf16[256,320]{0,1:T(8,128)(2,1)S(1)}, bf16[256,320]{0,1:T(8,128)(2,1)S(1)}, u32[]{:S(2)}, u32[]{:S(2)}) collective-permute-start(bf16[256,320]{0,1:T(8,128)(2,1)S(1)} %get-tuple-element.27), channel_id=1, source_target_pairs={{508,0},{0,4},{4,8},{8,12},{12,16},{16,20},{20,24},{24,28},{28,32}... | collective-permute-start | bytes 491528 | tf_op jit(solution)/shard_map/ppermute | solution.py:10
  139.5 6.6 %collective-permute-start.3 = (bf16[256,320]{0,1:T(8,128)(2,1)S(1)}, bf16[256,320]{0,1:T(8,128)(2,1)S(1)}, u32[]{:S(2)}, u32[]{:S(2)}) collective-permute-start(bf16[256,320]{0,1:T(8,128)(2,1)S(1)} %get-tuple-element.27), channel_id=1, source_target_pairs={{4,0},{8,4},{12,8},{16,12},{20,16},{24,20},{28,24},{32,28},{36,32}... | collective-permute-start | bytes 491528 | tf_op jit(solution)/shard_map/ppermute | solution.py:10
  141.6 4.5 %copy-start.2 = (f32[256,320]{0,1:T(8,128)S(1)}, f32[256,320]{0,1:T(8,128)}, u32[]{:S(2)}) copy-start(f32[256,320]{0,1:T(8,128)} %get-tuple-element.28) | copy-start | bytes 983044
  154.1 1.4 copy-start.45
  178.7 1.2 copy-start.10
  178.7 1.2 copy-start.49
  (16 other events, 13.2 us)
Sparse Core Ops, SparseCore 0:
  100.8 27.1 all-gather.2
  141.8 32.8 all-gather.4
where the time goes:
time: 189 us; the launch traced here: 188 us
  waiting for transfers between devices  76.4 us (40%)
  starting transfers between devices  43 us (23%)
  local copies, waits for them, and re-layouts  39.3 us (21%)
  between operations  14.9 us (8%)
  other arithmetic  8.01 us (4%)
  matrix products  6.58 us (3%)
    all_gather x2, waiting for transfers between devices, body(): group_pool = lax.all_gather(result, 'grp', axis=0, tiled=True)  24.7 us
    all_to_all x1, waiting for transfers between devices, body(): lax.all_to_all(pack_rows(adjoint_rhs, send_slot), 'blk', split_axis=0, co...  23.6 us
    all_to_all x1, waiting for transfers between devices, body(): lax.all_to_all(pack_rows(checkpoint, send_slot), 'blk', split_axis=0, con...  21.9 us
    all_to_all x1, starting transfers between devices, body(): lax.all_to_all(pack_rows(checkpoint, send_slot), 'blk', split_axis=0, con...  20.5 us
    gather x12, local copies, waits for them, and re-layouts, face_sum(): jnp.take(block_pool, face_index[face_id], axis=0)  13.4 us
    ppermute x4, starting transfers between devices, passed_along(): return lax.ppermute(block, axis, route)  13.3 us
    all_to_all x1, starting transfers between devices, body(): lax.all_to_all(pack_rows(adjoint_rhs, send_slot), 'blk', split_axis=0, co...  8.93 us
    ppermute x4, waiting for transfers between devices, passed_along(): return lax.ppermute(block, axis, route)  6.07 us
  transfers between devices with their start and end apart: 8, of which 6 were waited for; matrix products, arithmetic and copies ran while one was open for 17% of the time, Pallas kernels for 0%

commit v1 on v0

v1 whole, which is shorter than its diff:
```python
import jax
import jax.numpy as jnp
from jax import lax
from jax.experimental import pallas as pl
from jax.experimental.pallas import tpu as pltpu
from jax.sharding import PartitionSpec as P

MESH = pl.DeviceIdType.MESH
ROWS = 256
VALS = 320
PADDED = 384
PACKED = 640
BLK = 128
GRP = 4
NZ = 16
ND = 8
CAP = 4
SLOTS = BLK * CAP
DONORS = 128
CHUNKS = 4
CHUNK = SLOTS // CHUNKS
F32 = jnp.float32
BF16 = jnp.bfloat16
ORDER = (8, 9, 7, 10, 6, 11, 5, 12, 4, 13, 3, 14, 2, 15, 1, 0)


def dot(a, b):
    return jnp.dot(a, b, preferred_element_type=F32)


def iota(shape, dim):
    return lax.broadcasted_iota(jnp.int32, shape, dim)


def piece_of(blk, me):
    away = (blk // ND - me // ND) & (NZ - 1)
    place = jnp.where(away == 0, NZ - 1, jnp.where(away <= NZ // 2, NZ - 2 * away, 2 * away - NZ - 1))
    return place, (blk - me) & (ND - 1)


def kernel(
    ckpt, rhs, npos, opos, lmat, rmat, fblk, fw, dblk, dw, out,
    send, zrecv, zpack, got, table, onehot, donor_hot, pool, donor_pool, mats_a, mats_b,
    left_gain, right_gain, inv_diag, rhs_f, value,
    zs_sem, zr_sem, ds_sem, dr_sem, hs_sem, hr_sem,
):
    me = lax.axis_index("blk")
    grp = lax.axis_index("grp")
    my_z, my_d = me // ND, me % ND
    below, above = (me + BLK - 1) % BLK, (me + 1) % BLK

    barrier = pltpu.get_barrier_semaphore()

    def greet(**where):
        pl.semaphore_signal(barrier, inc=1, device_id=where, device_id_type=MESH)

    for away in ORDER[:-1]:
        greet(blk=(my_z + away) % NZ * ND + my_d)
    for e in range(1, ND):
        greet(blk=my_z * ND + (my_d + e) % ND)
    for g in range(1, GRP):
        greet(grp=(grp + g) % GRP)
    greet(blk=below)
    greet(blk=above)

    target = npos[...] >> 10
    place, e = piece_of(target, me)
    key = place * ND + (((target & (ND - 1)) - my_d) & (ND - 1))
    hot = (key == iota((BLK, ROWS), 0)).astype(BF16)
    before = (iota((ROWS, ROWS), 0) < iota((ROWS, ROWS), 1)).astype(BF16)
    rank = jnp.sum(hot.astype(F32) * dot(hot, before), axis=0, keepdims=True)
    slot = (key * CAP).astype(F32) + rank
    put = (slot == iota((SLOTS, ROWS), 0).astype(F32)).astype(BF16)
    tail = jnp.concatenate([ckpt[:, 256:VALS], rhs[:, 256:VALS]], axis=1)
    send[:, 0:256] = dot(put, ckpt[:, 0:256]).astype(BF16)
    send[:, 256:512] = dot(put, rhs[:, 0:256]).astype(BF16)
    send[:, 512:640] = dot(put, tail).astype(BF16)

    pl.semaphore_wait(barrier, NZ - 1 + ND - 1 + GRP - 1 + 2)

    piece = ND * CAP
    z_copies = []
    for p, away in enumerate(ORDER[:-1]):
        rows = pl.ds(p * piece, piece)
        z_copies.append(
            pltpu.make_async_remote_copy(
                src_ref=send.at[rows],
                dst_ref=zrecv.at[rows],
                send_sem=zs_sem.at[p],
                recv_sem=zr_sem.at[p],
                device_id={"blk": (my_z + away) % NZ * ND + my_d},
                device_id_type=MESH,
            )
        )
        z_copies[-1].start()
    own = pl.ds((NZ - 1) * piece, piece)
    zrecv[own, :] = send[own, :]

    table[...] = jnp.zeros_like(table)
    faces = fblk[...]
    face_place = (((faces >> 10) - me + 1) & (BLK - 1)) * ROWS + (faces & (ROWS - 1))
    table[0:6, :] = jnp.where(faces >= 0, face_place, -1).astype(F32)
    table[8:14, :] = fw[...]
    donors = dblk[...]
    donor_place = ((((donors >> 8) - grp) & (GRP - 1)) - 1) * DONORS + (donors & (ROWS - 1))
    table[16:18, :] = donor_place.astype(F32)
    table[24:26, :] = dw[...]
    anchor = opos[...] >> 10
    place, e = piece_of(anchor, me)
    e = (my_d - (anchor & (ND - 1))) & (ND - 1)
    away = (my_z - anchor // ND) & (NZ - 1)
    place = jnp.where(away == 0, NZ - 1, jnp.where(away <= NZ // 2, NZ - 2 * away, 2 * away - NZ - 1))
    order_row = ((place * ND + e) * ROWS + (opos[...] & (ROWS - 1))).astype(F32)
    base = (place >> 2) * CHUNK + e * 16 + (place & 3) * CAP
    table[32:33, :] = order_row
    table[40:41, :] = base.astype(F32)
    columns = jnp.transpose(table[...])

    def column(n):
        return columns[:, n : n + 1]

    smaller = (order_row < column(32)).astype(BF16)
    rank = dot(smaller, jnp.ones((ROWS, 128), BF16)).astype(jnp.int32) & (CAP - 1)
    recv_slot = rank.astype(F32) + column(40)
    lanes = iota((ROWS, 128), 1).astype(F32)
    pick = jnp.concatenate(
        [(recv_slot == lanes + 128.0 * t).astype(BF16) for t in range(SLOTS // 128)], axis=1
    )
    pool_lane = iota((ROWS, 3 * ROWS), 1).astype(F32)
    for f in range(6):
        onehot[f * ROWS : (f + 1) * ROWS, :] = (column(f) == pool_lane).astype(BF16)
    donor_lane = iota((ROWS, 3 * DONORS), 1).astype(F32)
    for k in range(2):
        donor_hot[k * ROWS : (k + 1) * ROWS, :] = (column(16 + k) == donor_lane).astype(BF16)

    mats_a[...] = jnp.zeros_like(mats_a)
    mats_b[...] = jnp.zeros_like(mats_b)
    mats_a[0:VALS, 0:VALS] = lmat[...]
    mats_b[0:VALS, 0:VALS] = rmat[...]
    mats_a[:, PADDED:] = jnp.transpose(mats_b[0:PADDED, :])
    mats_b[PADDED:, :] = jnp.transpose(mats_a[:, 0:PADDED])

    row, col = iota((CHUNK, CHUNK), 0), iota((CHUNK, CHUNK), 1)
    regroup = (col == ((row >> 2) & 3) * piece + (row >> 4) * CAP + (row & 3)).astype(BF16)
    d_copies = []
    per = CHUNK // ND
    for q in range(CHUNKS):
        for p in range(4 * q, min(4 * q + 4, NZ - 1)):
            z_copies[p].wait_recv()
        rows = slice(q * CHUNK, (q + 1) * CHUNK)
        moved = dot(regroup, zrecv[rows, :]).astype(BF16)
        zpack[rows, :] = moved
        for e in range(1, ND):
            part = pl.ds(q * CHUNK + e * per, per)
            d_copies.append(
                pltpu.make_async_remote_copy(
                    src_ref=zpack.at[part],
                    dst_ref=got.at[part],
                    send_sem=ds_sem.at[q * (ND - 1) + e - 1],
                    recv_sem=dr_sem.at[q * (ND - 1) + e - 1],
                    device_id={"blk": my_z * ND + (my_d + e) % ND},
                    device_id_type=MESH,
                )
            )
            d_copies[-1].start()
        got[q * CHUNK : q * CHUNK + per, :] = moved[0:per, :]
    for copy in d_copies:
        copy.wait_recv()

    valid = iota((ROWS, 128), 1) < 64
    last = dot(pick, got[:, 512:640])
    state = jnp.concatenate([dot(pick, got[:, 0:256]), jnp.where(valid, last, 0.0)], axis=1)
    diag = 1.0 / (2.0 + state * state)
    inv_diag[...] = diag
    rhs_new = jnp.concatenate(
        [dot(pick, got[:, 256:512]), jnp.where(valid, pltpu.roll(last, 64, 1), 0.0)], axis=1
    )
    rhs_f[...] = rhs_new
    first = rhs_new * diag
    value[...] = first
    left_gain[...] = 0.5 * jnp.tanh(state)
    right_gain[...] = 0.4 * jnp.tanh(1.5 * state - 0.5)

    lane = iota((ROWS, 128), 1)

    def sweep(s, carry):
        rounded = value[...].astype(BF16)
        pool[s, ROWS : 2 * ROWS, :] = rounded
        copies = []
        for n, (where, dst) in enumerate(((above, 0), (below, 2 * ROWS))):
            copies.append(
                pltpu.make_async_remote_copy(
                    src_ref=pool.at[s, pl.ds(ROWS, ROWS)],
                    dst_ref=pool.at[s, pl.ds(dst, ROWS)],
                    send_sem=hs_sem.at[s, n],
                    recv_sem=hr_sem.at[s, n],
                    device_id={"blk": where},
                    device_id_type=MESH,
                )
            )
        for g in range(1, GRP):
            copies.append(
                pltpu.make_async_remote_copy(
                    src_ref=pool.at[s, pl.ds(ROWS, DONORS)],
                    dst_ref=donor_pool.at[s, pl.ds((g - 1) * DONORS, DONORS)],
                    send_sem=hs_sem.at[s, 1 + g],
                    recv_sem=hr_sem.at[s, 1 + g],
                    device_id={"grp": (grp + GRP - g) % GRP},
                    device_id_type=MESH,
                )
            )
        for copy in copies:
            copy.start()

        proj = dot(rounded, mats_a[...])
        mid_l = (proj[:, 0:PADDED] * left_gain[...]).astype(BF16)
        mid_r = (proj[:, PADDED:] * right_gain[...]).astype(BF16)
        applied = dot(mid_l, mats_b[0:PADDED, :]) + dot(mid_r, mats_b[PADDED:, :])
        value[...] = rhs_f[...] - applied

        for copy in copies:
            copy.wait_recv()
        tiles = [jnp.zeros((ROWS, 128), F32) for _ in range(3)]
        for f in range(6):
            stride = (16, 4, 1)[f // 2]
            cell = lane // stride % 4
            fetched = dot(onehot[f * ROWS : (f + 1) * ROWS, :], pool[s]) * table_t(f)
            for t in range(3):
                tile = fetched[:, 128 * t : 128 * t + 128]
                if f % 2 == 0:
                    moved = jnp.where(cell == 0, pltpu.roll(tile, 128 - 3 * stride, 1), 0.0)
                else:
                    moved = jnp.where(cell == 3, pltpu.roll(tile, 3 * stride, 1), 0.0)
                tiles[t] = tiles[t] + moved
        total = jnp.concatenate(tiles, axis=1)
        donor = dot(donor_hot[...], donor_pool[s])
        fringe = donor[0:ROWS] * column(24) + donor[ROWS:] * column(25)
        value[...] = ((value[...] - total) - fringe) * inv_diag[...]
        for copy in copies:
            copy.wait_send()
        return carry

    def table_t(f):
        return column(8 + f)

    lax.fori_loop(0, 2, sweep, 0)
    out[...] = value[:, 0:VALS]
    for copy in z_copies + d_copies:
        copy.wait_send()


def body(ckpt, rhs, npos, opos, lmat, rmat, fblk, fw, dblk, dw):
    vmem = pl.BlockSpec(memory_space=pltpu.VMEM)
    dma = pltpu.SemaphoreType.DMA
    return pl.pallas_call(
        kernel,
        out_shape=jax.ShapeDtypeStruct((ROWS, VALS), F32),
        in_specs=[vmem] * 10,
        out_specs=vmem,
        scratch_shapes=[
            pltpu.VMEM((SLOTS, PACKED), BF16),
            pltpu.VMEM((SLOTS, PACKED), BF16),
            pltpu.VMEM((SLOTS, PACKED), BF16),
            pltpu.VMEM((SLOTS, PACKED), BF16),
            pltpu.VMEM((128, ROWS), F32),
            pltpu.VMEM((6 * ROWS, 3 * ROWS), BF16),
            pltpu.VMEM((2 * ROWS, 3 * DONORS), BF16),
            pltpu.VMEM((2, 3 * ROWS, PADDED), BF16),
            pltpu.VMEM((2, 3 * DONORS, PADDED), BF16),
            pltpu.VMEM((PADDED, 2 * PADDED), BF16),
            pltpu.VMEM((2 * PADDED, PADDED), BF16),
        ]
        + [pltpu.VMEM((ROWS, PADDED), F32)] * 5
        + [
            dma((NZ - 1,)), dma((NZ - 1,)),
            dma((CHUNKS * (ND - 1),)), dma((CHUNKS * (ND - 1),)),
            dma((2, 5)), dma((2, 5)),
        ],
        compiler_params=pltpu.CompilerParams(collective_id=0, has_side_effects=True),
    )(ckpt, rhs, npos.reshape(1, ROWS), opos.reshape(1, ROWS), lmat, rmat, fblk, fw, dblk, dw)


def solution(mesh):
    row, vec, many = P(("blk", "grp"), None), P(("blk", "grp")), P(None, ("blk", "grp"))
    return jax.shard_map(
        body,
        mesh=mesh,
        in_specs=(row, row, vec, vec, P(), P(), many, many, many, many),
        out_specs=row,
        check_vma=False,
    )
```

time: 189 us -> 76.8 us (0.41)
  waiting for transfers between devices: 76.4 us -> 0 us
  Pallas kernels: 0 us -> 72.2 us
  starting transfers between devices: 43 us -> 0 us
  local copies, waits for them, and re-layouts: 39.3 us -> 4.46 us
  between operations: 14.9 us -> 0.01 us
  other arithmetic: 8.01 us -> 0 us
  matrix products: 6.58 us -> 0 us
    pallas_call x0 -> x1, Pallas kernels: none -> 72.2 us  [body(): pl.pallas_call(kernel, out_shape=jax.ShapeDtypeStruct((ROWS, VALS), F32),...]
    all_to_all x2 -> x0, waiting for transfers between devices: 45.5 us -> none  [the longest x1 23.6 us: body(): lax.all_to_all(pack_rows(adjoint_rhs, send_slot), 'blk', split_axis=0, co...]
    all_to_all x2 -> x0, starting transfers between devices: 29.4 us -> none  [the longest x1 20.5 us: body(): lax.all_to_all(pack_rows(checkpoint, send_slot), 'blk', split_axis=0, con...]
    all_gather x2 -> x0, waiting for transfers between devices: 24.7 us -> none  [body(): group_pool = lax.all_gather(result, 'grp', axis=0, tiled=True)]
    gather x24 -> x0, local copies, waits for them, and re-layouts: 20.8 us -> none  [the longest x12 13.4 us: face_sum(): jnp.take(block_pool, face_index[face_id], axis=0)]
    ppermute x4 -> x0, starting transfers between devices: 13.3 us -> none  [passed_along(): return lax.ppermute(block, axis, route)]
    dot_general x4 -> x0, matrix products: 6.58 us -> none  [the longest x2 3.84 us: transposed_apply(): jnp.dot(second_mid, left_trans, preferred_element_type=jnp.float32)]
    ppermute x4 -> x0, waiting for transfers between devices: 6.07 us -> none  [passed_along(): return lax.ppermute(block, axis, route)]
  transfers between devices with their start and end apart: 8 -> 0, of which waited for: 6 -> 0; matrix products, arithmetic and copies ran while one was open for 17% -> 0% of each run, Pallas kernels for 0% -> 0%
where the time goes in v1:
time: 76.8 us; the launch traced here: 76.7 us
  Pallas kernels  72.2 us (94%)
  local copies, waits for them, and re-layouts  4.46 us (6%)
    pallas_call x1, Pallas kernels, body(): pl.pallas_call(kernel, out_shape=jax.ShapeDtypeStruct((ROWS, VALS), F32),...  72.2 us
    unnamed x4, local copies, waits for them, and re-layouts  2.59 us
    pallas_call x1, local copies, waits for them, and re-layouts, body(): pl.pallas_call(kernel, out_shape=jax.ShapeDtypeStruct((ROWS, VALS), F32),...  1.87 us

profile of v1, /device:TPU:1, one launch (start us, length us, event | category | flops | bytes accessed | tf_op | source)
XLA Modules:
  0.0 76.7 jit_solution(15056705992892393249)
XLA Ops:
  0.0 0.0 copy-start
  0.0 1.8 %copy.11.ckpt = bf16[256,320]{1,0:T(8,128)(2,1)} copy(bf16[256,320]{0,1:T(8,128)(2,1)} %param.10) | data formatting | bytes 327680 | tf_op args[0]
  1.8 0.0 copy-done
  1.8 0.8 %copy.12.rhs = bf16[256,320]{1,0:T(8,128)(2,1)} copy(bf16[256,320]{0,1:T(8,128)(2,1)S(1)} %copy-done) | data formatting | bytes 327680 | tf_op args[1]
  2.6 72.2 %shard_map.100 = f32[256,320]{1,0:T(8,128)} custom-call(bf16[256,320]{1,0:T(8,128)(2,1)} %copy.11.ckpt, bf16[256,320]{1,0:T(8,128)(2,1)} %copy.12.rhs, s32[1,256]{1,0:T(1,128)} %bitcast.2, s32[1,256]{1,0:T(1,128)} %bitcast.3, bf16[320,320]{1,0:T(8,128)(2,1)} %lmat.1, bf16[320,320]{1,0:T(8,128)(2,1)} %rmat.1, s32[6,256]{1,0:T(8,128)} %fblk.1, f32[6,256]{1,0:T(8,128)} %fw.1, ...), custom_call_target="tpu_custom_call" | custom-call | tf_op jit(solution)/shard_map/pallas_call | solution.py:255
  74.8 1.9 %copy.13 = f32[256,320]{0,1:T(8,128)} copy(f32[256,320]{1,0:T(8,128)} %shard_map.100) | data formatting | bytes 655360 | tf_op jit(solution)/shard_map/pallas_call | solution.py:255
Async XLA Ops:
  0.0 1.8 %copy-start = (bf16[256,320]{0,1:T(8,128)(2,1)S(1)}, bf16[256,320]{0,1:T(8,128)(2,1)}, u32[]{:S(2)}) copy-start(bf16[256,320]{0,1:T(8,128)(2,1)} %param.11) | copy-start | bytes 491524

commit v2 on v1

v2 whole, which is shorter than its diff:
```python
import jax
import jax.numpy as jnp
from jax import lax
from jax.experimental import pallas as pl
from jax.experimental.pallas import tpu as pltpu
from jax.sharding import PartitionSpec as P

MESH = pl.DeviceIdType.MESH
ROWS = 256
VALS = 320
MAIN = 256
PADDED = 384
PACKED = 640
BLK = 128
GRP = 4
NZ = 16
ND = 8
CAP = 4
SLOTS = BLK * CAP
DONORS = 128
PER_CHUNK = 2
CHUNKS = NZ // PER_CHUNK
CHUNK = SLOTS // CHUNKS
PIECE = ND * CAP
PART = PER_CHUNK * CAP
F32 = jnp.float32
BF16 = jnp.bfloat16
ORDER = (0, 1, 15, 8, 9, 7, 10, 6, 11, 5, 12, 4, 13, 3, 14, 2)


def dot(a, b):
    return jnp.dot(a, b, preferred_element_type=F32)


def dot_t(a, b):
    return lax.dot_general(a, b, (((1,), (1,)), ((), ())), preferred_element_type=F32)


def iota(shape, dim):
    return lax.broadcasted_iota(jnp.int32, shape, dim)


def place_of(away):
    away = away & (NZ - 1)
    far = jnp.where(away <= NZ // 2, NZ + 3 - 2 * away, 2 * away - NZ + 2)
    return jnp.where(away <= 1, away, jnp.where(away == NZ - 1, 2, far))


def remote(src, dst, send_sem, recv_sem, **where):
    return pltpu.make_async_remote_copy(
        src_ref=src, dst_ref=dst, send_sem=send_sem, recv_sem=recv_sem, device_id=where, device_id_type=MESH
    )


def kernel(
    ckpt_hbm, rhs_hbm, npos_hbm, opos_hbm, lmat_hbm, rmat_hbm, fblk_hbm, fw_hbm, dblk_hbm, dw_hbm, out,
    ckpt, rhs, npos, opos, lmat, rmat, fblk, fw, dblk, dw,
    send, zrecv, zpack, got, table, onehot, donor_hot,
    pool, pool_tail, own_tail, halo_tail, donor_pool, donor_tail, donor_in, mats_a, mats_b,
    left_gain, right_gain, inv_diag, rhs_f, value,
    in_sem, zs_sem, zr_sem, ds_sem, dr_sem, hs_sem, hr_sem,
):
    me = lax.axis_index("blk")
    grp = lax.axis_index("grp")
    my_z, my_d = me // ND, me % ND
    below, above = (me + BLK - 1) % BLK, (me + 1) % BLK

    barrier = pltpu.get_barrier_semaphore()

    def greet(**where):
        pl.semaphore_signal(barrier, inc=1, device_id=where, device_id_type=MESH)

    for away in (8, 7, 9, 6, 10, 5, 11, 4, 12, 3, 13, 2, 14, 1, 15):
        greet(blk=(my_z + away) % NZ * ND + my_d)
    for e in range(1, ND):
        greet(blk=my_z * ND + (my_d + e) % ND)
    for g in range(1, GRP):
        greet(grp=(grp + g) % GRP)
    greet(blk=below)
    greet(blk=above)

    pairs = (
        (npos_hbm, npos), (ckpt_hbm, ckpt), (rhs_hbm, rhs), (opos_hbm, opos), (fblk_hbm, fblk),
        (fw_hbm, fw), (dblk_hbm, dblk), (dw_hbm, dw), (lmat_hbm, lmat), (rmat_hbm, rmat),
    )
    loads = [pltpu.make_async_copy(a, b, in_sem.at[i]) for i, (a, b) in enumerate(pairs)]
    for load in loads:
        load.start()

    loads[0].wait()
    target = npos[...] >> 10
    key = place_of((target >> 3) - my_z) * ND + (((target & (ND - 1)) - my_d) & (ND - 1))
    hot = (key == iota((BLK, ROWS), 0)).astype(BF16)
    earlier = (iota((ROWS, ROWS), 0) < iota((ROWS, ROWS), 1)).astype(BF16)
    rank = jnp.sum(hot.astype(F32) * dot(hot, earlier), axis=0, keepdims=True)
    slot = (key * CAP).astype(F32) + rank
    put = (slot == iota((SLOTS, ROWS), 0).astype(F32)).astype(BF16)
    loads[1].wait()
    loads[2].wait()
    tail = jnp.concatenate([ckpt[MAIN:VALS, :], rhs[MAIN:VALS, :]], axis=0)
    send[:, 0:256] = dot_t(put, ckpt[0:MAIN, :]).astype(BF16)
    send[:, 256:512] = dot_t(put, rhs[0:MAIN, :]).astype(BF16)
    send[:, 512:640] = dot_t(put, tail).astype(BF16)

    pl.semaphore_wait(barrier, NZ - 1 + ND - 1 + GRP - 1 + 2)

    z_copies = [None]
    for p in range(1, NZ):
        rows = pl.ds(p * PIECE, PIECE)
        z_copies.append(
            remote(
                send.at[rows], zrecv.at[rows], zs_sem.at[p - 1], zr_sem.at[p - 1],
                blk=(my_z + ORDER[p]) % NZ * ND + my_d,
            )
        )
        z_copies[-1].start()
    zrecv[0:PIECE, :] = send[0:PIECE, :]

    row, col = iota((CHUNK, CHUNK), 0), iota((CHUNK, CHUNK), 1)
    regroup = (col == ((row // CAP) % PER_CHUNK) * PIECE + (row // PART) * CAP + row % CAP).astype(BF16)
    d_copies = []

    def pass_on(q):
        for p in range(PER_CHUNK * q, PER_CHUNK * (q + 1)):
            if p:
                z_copies[p].wait_recv()
        rows = slice(q * CHUNK, (q + 1) * CHUNK)
        moved = dot(regroup, zrecv[rows, :]).astype(BF16)
        zpack[rows, :] = moved
        for e in (4, 5, 3, 2, 6, 7, 1):
            part = pl.ds(q * CHUNK + e * PART, PART)
            n = q * (ND - 1) + e - 1
            d_copies.append(
                remote(
                    zpack.at[part], got.at[part], ds_sem.at[n], dr_sem.at[n],
                    blk=my_z * ND + (my_d + e) % ND,
                )
            )
            d_copies[-1].start()
        got[q * CHUNK : q * CHUNK + PART, :] = moved[0:PART, :]

    for load in loads[3:]:
        load.wait()
    table[...] = jnp.zeros_like(table)
    faces = fblk[...]
    face_place = (((faces >> 10) - me + 1) & (BLK - 1)) * ROWS + (faces & (ROWS - 1))
    table[0:6, :] = jnp.where(faces >= 0, face_place, -1).astype(F32)
    table[8:14, :] = fw[...]
    donors = dblk[...]
    donor_place = ((((donors >> 8) - grp) & (GRP - 1)) - 1) * DONORS + (donors & (ROWS - 1))
    table[16:18, :] = donor_place.astype(F32)
    table[24:26, :] = dw[...]
    anchor = opos[...] >> 10
    e = (my_d - (anchor & (ND - 1))) & (ND - 1)
    place = place_of(my_z - (anchor >> 3))
    order_row = ((place * ND + e) * ROWS + (opos[...] & (ROWS - 1))).astype(F32)
    base = (place // PER_CHUNK) * CHUNK + e * PART + (place % PER_CHUNK) * CAP
    table[32:33, :] = order_row
    table[40:41, :] = base.astype(F32)
    columns = jnp.transpose(table[...])

    def column(n):
        return columns[:, n : n + 1]

    smaller = (order_row < column(32)).astype(BF16)
    rank = dot(smaller, jnp.ones((ROWS, 128), BF16)).astype(jnp.int32) & (CAP - 1)
    recv_slot = rank.astype(F32) + column(40)
    lanes = iota((ROWS, 128), 1).astype(F32)
    pick = jnp.concatenate(
        [(recv_slot == lanes + 128.0 * t).astype(BF16) for t in range(SLOTS // 128)], axis=1
    )
    pool_lane = iota((ROWS, 3 * ROWS), 1).astype(F32)
    for f in range(6):
        onehot[f * ROWS : (f + 1) * ROWS, :] = (column(f) == pool_lane).astype(BF16)
    donor_lane = iota((ROWS, 3 * DONORS), 1).astype(F32)
    for k in range(2):
        donor_hot[k * ROWS : (k + 1) * ROWS, :] = (column(16 + k) == donor_lane).astype(BF16)

    mats_a[...] = jnp.zeros_like(mats_a)
    mats_b[...] = jnp.zeros_like(mats_b)
    mats_a[0:VALS, 0:VALS] = lmat[...]
    mats_b[0:VALS, 0:VALS] = rmat[...]
    mats_a[:, PADDED:] = jnp.transpose(mats_b[0:PADDED, :])
    mats_b[PADDED:, :] = jnp.transpose(mats_a[:, 0:PADDED])

    for q in range(CHUNKS):
        pass_on(q)
    for copy in d_copies:
        copy.wait_recv()

    half = iota((ROWS, 128), 1) < 64
    last = dot(pick, got[:, 512:640])
    state = jnp.concatenate([dot(pick, got[:, 0:256]), jnp.where(half, last, 0.0)], axis=1)
    diag = 1.0 / (2.0 + state * state)
    inv_diag[...] = diag
    rhs_new = jnp.concatenate(
        [dot(pick, got[:, 256:512]), jnp.where(half, pltpu.roll(last, 64, 1), 0.0)], axis=1
    )
    rhs_f[...] = rhs_new
    value[...] = rhs_new * diag

    def stage(s, h, rows):
        at = ROWS + DONORS * h
        pool[s, at : at + DONORS, :] = rows[:, 0:MAIN].astype(BF16)
        tails = rows[:, MAIN:]
        pool_tail[s, at : at + DONORS, :] = tails.astype(BF16)
        both = jnp.where(half[0:64], tails[0:64], pltpu.roll(tails[64:128], 64, 1))
        own_tail[s, 64 * h : 64 * h + 64, :] = both.astype(BF16)

    def send_donors(s):
        copies = []
        for g in (2, 1, 3):
            n = 4 + 2 * (g - 1)
            to = (grp + GRP - g) % GRP
            copies.append(
                remote(
                    pool.at[s, pl.ds(ROWS, DONORS)], donor_pool.at[s, pl.ds((g - 1) * DONORS, DONORS)],
                    hs_sem.at[s, n], hr_sem.at[s, n], grp=to,
                )
            )
            copies.append(
                remote(
                    own_tail.at[s, pl.ds(0, 64)], donor_in.at[s, pl.ds((g - 1) * 64, 64)],
                    hs_sem.at[s, n + 1], hr_sem.at[s, n + 1], grp=to,
                )
            )
        for copy in copies:
            copy.start()
        return copies

    def send_halo(s):
        copies = []
        for n, (to, dst) in enumerate(((above, 0), (below, 2))):
            copies.append(
                remote(
                    pool.at[s, pl.ds(ROWS, ROWS)], pool.at[s, pl.ds(dst * ROWS, ROWS)],
                    hs_sem.at[s, 2 * n], hr_sem.at[s, 2 * n], blk=to,
                )
            )
            copies.append(
                remote(
                    own_tail.at[s], halo_tail.at[s, n],
                    hs_sem.at[s, 2 * n + 1], hr_sem.at[s, 2 * n + 1], blk=to,
                )
            )
        for copy in copies:
            copy.start()
        return copies

    def spread(packed):
        wide = packed.astype(F32)
        return packed, pltpu.roll(wide, 64, 1).astype(BF16)

    stage(0, 0, value[0:DONORS, :])
    donor_copies = send_donors(0)
    stage(0, 1, value[DONORS:, :])
    halo_copies = send_halo(0)
    left_gain[...] = 0.5 * jnp.tanh(state)
    right_gain[...] = 0.4 * jnp.tanh(1.5 * state - 0.5)

    lane = iota((ROWS, 128), 1)
    for s in range(2):
        rounded = value[...].astype(BF16)
        proj = dot(rounded, mats_a[...])
        mid_l = (proj[:, 0:PADDED] * left_gain[...]).astype(BF16)
        mid_r = (proj[:, PADDED:] * right_gain[...]).astype(BF16)
        applied = dot(mid_l, mats_b[0:PADDED, :]) + dot(mid_r, mats_b[PADDED:, :])
        value[...] = rhs_f[...] - applied

        for copy in halo_copies:
            copy.wait_recv()
        for n, dst in enumerate((0, 2 * ROWS)):
            for h in range(2):
                even, odd = spread(halo_tail[s, n, 64 * h : 64 * h + 64, :])
                at = dst + DONORS * h
                pool_tail[s, at : at + 64, :] = even
                pool_tail[s, at + 64 : at + 128, :] = odd
        tiles = [jnp.zeros((ROWS, 128), F32) for _ in range(3)]
        for f in range(6):
            stride = (16, 4, 1)[f // 2]
            cell = lane // stride % 4
            hot = onehot[f * ROWS : (f + 1) * ROWS, :]
            weight = column(8 + f)
            fetched = dot(hot, pool[s]) * weight
            parts = (fetched[:, 0:128], fetched[:, 128:256], dot(hot, pool_tail[s]) * weight)
            for t in range(3):
                if f % 2 == 0:
                    moved = jnp.where(cell == 0, pltpu.roll(parts[t], 128 - 3 * stride, 1), 0.0)
                else:
                    moved = jnp.where(cell == 3, pltpu.roll(parts[t], 3 * stride, 1), 0.0)
                tiles[t] = tiles[t] + moved
        value[...] = value[...] - jnp.concatenate(tiles, axis=1)

        for copy in donor_copies:
            copy.wait_recv()
        for g in range(GRP - 1):
            even, odd = spread(donor_in[s, 64 * g : 64 * g + 64, :])
            donor_tail[s, DONORS * g : DONORS * g + 64, :] = even
            donor_tail[s, DONORS * g + 64 : DONORS * g + 128, :] = odd
        done = donor_copies + halo_copies
        donor = jnp.concatenate([dot(donor_hot[...], donor_pool[s]), dot(donor_hot[...], donor_tail[s])], axis=1)
        fringe = donor[0:ROWS] * column(24) + donor[ROWS:] * column(25)
        value[...] = (value[...] - fringe) * inv_diag[...]
        if s == 0:
            stage(1, 0, value[0:DONORS, :])
            donor_copies = send_donors(1)
            stage(1, 1, value[DONORS:, :])
            halo_copies = send_halo(1)
        for copy in done:
            copy.wait_send()
    out[...] = jnp.transpose(value[...])[0:VALS, :]
    for copy in z_copies[1:] + d_copies:
        copy.wait_send()


def body(ckpt, rhs, npos, opos, lmat, rmat, fblk, fw, dblk, dw):
    args = (ckpt.T, rhs.T, npos.reshape(1, ROWS), opos.reshape(1, ROWS), lmat, rmat, fblk, fw, dblk, dw)
    dma = pltpu.SemaphoreType.DMA
    out = pl.pallas_call(
        kernel,
        out_shape=pltpu.VMEM((VALS, ROWS), F32),
        in_specs=[pl.BlockSpec(memory_space=pl.ANY)] * 10,
        out_specs=pl.BlockSpec(memory_space=pltpu.VMEM),
        scratch_shapes=[pltpu.VMEM(a.shape, a.dtype) for a in args]
        + [pltpu.VMEM((SLOTS, PACKED), BF16)] * 4
        + [
            pltpu.VMEM((128, ROWS), F32),
            pltpu.VMEM((6 * ROWS, 3 * ROWS), BF16),
            pltpu.VMEM((2 * ROWS, 3 * DONORS), BF16),
            pltpu.VMEM((2, 3 * ROWS, MAIN), BF16),
            pltpu.VMEM((2, 3 * ROWS, 128), BF16),
            pltpu.VMEM((2, DONORS, 128), BF16),
            pltpu.VMEM((2, 2, DONORS, 128), BF16),
            pltpu.VMEM((2, 3 * DONORS, MAIN), BF16),
            pltpu.VMEM((2, 3 * DONORS, 128), BF16),
            pltpu.VMEM((2, 3 * 64, 128), BF16),
            pltpu.VMEM((PADDED, 2 * PADDED), BF16),
            pltpu.VMEM((2 * PADDED, PADDED), BF16),
        ]
        + [pltpu.VMEM((ROWS, PADDED), F32)] * 5
        + [dma((len(args),))]
        + [dma((NZ - 1,))] * 2
        + [dma((CHUNKS * (ND - 1),))] * 2
        + [dma((2, 10))] * 2,
        compiler_params=pltpu.CompilerParams(collective_id=0, has_side_effects=True),
    )(*args)
    return out.T


def solution(mesh):
    row, vec, many = P(("blk", "grp"), None), P(("blk", "grp")), P(None, ("blk", "grp"))
    return jax.shard_map(
        body,
        mesh=mesh,
        in_specs=(row, row, vec, vec, P(), P(), many, many, many, many),
        out_specs=row,
        check_vma=False,
    )
```

time: 76.8 us -> 67.9 us (0.88)
  Pallas kernels: 72.2 us -> 66.8 us
  local copies, waits for them, and re-layouts: 4.46 us -> 0.73 us
    pallas_call x1, Pallas kernels: 72.2 us -> 66.8 us  [body(): pl.pallas_call(kernel, out_shape=pltpu.VMEM((VALS, ROWS), F32), in_specs=...]
    pallas_call x1 -> x0, local copies, waits for them, and re-layouts: 1.87 us -> none  [body(): pl.pallas_call(kernel, out_shape=jax.ShapeDtypeStruct((ROWS, VALS), F32),...]
    unnamed x4 -> x1, local copies, waits for them, and re-layouts: 2.59 us -> 0.73 us
where the time goes in v2:
time: 67.9 us; the launch traced here: 67.5 us
  Pallas kernels  66.8 us (98%)
  local copies, waits for them, and re-layouts  0.73 us (1%)
    pallas_call x1, Pallas kernels, body(): pl.pallas_call(kernel, out_shape=pltpu.VMEM((VALS, ROWS), F32), in_specs=...  66.8 us

profile of v2, /device:TPU:1, one launch (start us, length us, event | category | flops | bytes accessed | tf_op | source)
XLA Modules:
  0.0 67.5 jit_solution(12817447002235547502)
XLA Ops:
  0.0 66.8 %shard_map.100 = f32[320,256]{1,0:T(8,128)S(1)} custom-call(bf16[320,256]{1,0:T(8,128)(2,1)} %bitcast.6, bf16[320,256]{1,0:T(8,128)(2,1)} %bitcast.7, s32[1,256]{1,0:T(1,128)} %bitcast.8, s32[1,256]{1,0:T(1,128)} %bitcast.9, bf16[320,320]{1,0:T(8,128)(2,1)} %lmat_hbm.1, bf16[320,320]{1,0:T(8,128)(2,1)} %rmat_hbm.1, s32[6,256]{1,0:T(8,128)} %fblk_hbm.1, ...), custom_call_target="tpu_custom_call" | custom-call | tf_op jit(solution)/shard_map/pallas_call | solution.py:319
  66.8 0.7 %copy.12 = f32[256,320]{0,1:T(8,128)} copy(f32[256,320]{0,1:T(8,128)S(1)} %bitcast.5) | data formatting | bytes 655360

commit v3 on v2

v3 whole, which is shorter than its diff:
```python
import jax
import jax.numpy as jnp
from jax import lax
from jax.experimental import pallas as pl
from jax.experimental.pallas import tpu as pltpu
from jax.sharding import PartitionSpec as P

MESH = pl.DeviceIdType.MESH
ROWS = 256
VALS = 320
MAIN = 256
PADDED = 384
PACKED = 640
BLK = 128
GRP = 4
NZ = 16
ND = 8
CAP = 4
SLOTS = BLK * CAP
DONORS = 128
PER_CHUNK = 2
CHUNKS = NZ // PER_CHUNK
CHUNK = SLOTS // CHUNKS
PIECE = ND * CAP
PART = PER_CHUNK * CAP
F32 = jnp.float32
BF16 = jnp.bfloat16
ORDER = (0, 8, 9, 7, 10, 6, 11, 5, 12, 4, 13, 3, 15, 1, 14, 2)


def dot(a, b):
    return jnp.dot(a, b, preferred_element_type=F32)


def dot_t(a, b):
    return lax.dot_general(a, b, (((1,), (1,)), ((), ())), preferred_element_type=F32)


def iota(shape, dim):
    return lax.broadcasted_iota(jnp.int32, shape, dim)


def place_of(away):
    away = away & (NZ - 1)
    return sum(jnp.where(away == a, p, 0) for p, a in enumerate(ORDER) if p)


def arrived(ref, sem):
    pltpu.make_async_copy(ref, ref, sem).wait()


def remote(src, dst, send_sem, recv_sem, **where):
    return pltpu.make_async_remote_copy(
        src_ref=src, dst_ref=dst, send_sem=send_sem, recv_sem=recv_sem, device_id=where, device_id_type=MESH
    )


def kernel(
    ckpt_hbm, rhs_hbm, npos_hbm, opos_hbm, lmat_hbm, rmat_hbm, fblk_hbm, fw_hbm, dblk_hbm, dw_hbm, out,
    ckpt, rhs, npos, opos, lmat, rmat, fblk, fw, dblk, dw,
    send, zrecv, zpack, got, table,
    own_hot, own_tail_hot, halo_hot, halo_tail_hot, donor_hot, donor_tail_hot,
    own, own_tail, halo, halo_tail, donor_pool, donor_tail, mats_a, mats_b,
    left_gain, right_gain, inv_diag, rhs_f, value,
    in_sem, zs_sem, zr_sem, ds_sem, dr_sem, hs_sem, hr_sem,
):
    me = lax.axis_index("blk")
    grp = lax.axis_index("grp")
    my_z, my_d = me // ND, me % ND
    below, above = (me + BLK - 1) % BLK, (me + 1) % BLK

    barrier = pltpu.get_barrier_semaphore()

    def greet(**where):
        pl.semaphore_signal(barrier, inc=1, device_id=where, device_id_type=MESH)

    for away in (8, 7, 9, 6, 10, 5, 11, 4, 12, 3, 13, 2, 14, 1, 15):
        greet(blk=(my_z + away) % NZ * ND + my_d)
    for e in range(1, ND):
        greet(blk=my_z * ND + (my_d + e) % ND)
    for g in range(1, GRP):
        greet(grp=(grp + g) % GRP)
    greet(blk=below)
    greet(blk=above)

    pairs = (
        (npos_hbm, npos), (ckpt_hbm, ckpt), (rhs_hbm, rhs), (opos_hbm, opos), (fblk_hbm, fblk),
        (fw_hbm, fw), (dblk_hbm, dblk), (dw_hbm, dw), (lmat_hbm, lmat), (rmat_hbm, rmat),
    )
    loads = [pltpu.make_async_copy(a, b, in_sem.at[i]) for i, (a, b) in enumerate(pairs)]
    for load in loads:
        load.start()

    loads[0].wait()
    target = npos[...] >> 10
    key = place_of((target >> 3) - my_z) * ND + (((target & (ND - 1)) - my_d) & (ND - 1))
    hot = (key == iota((BLK, ROWS), 0)).astype(BF16)
    earlier = (iota((ROWS, ROWS), 0) < iota((ROWS, ROWS), 1)).astype(BF16)
    rank = jnp.sum(hot.astype(F32) * dot(hot, earlier), axis=0, keepdims=True)
    slot = (key * CAP).astype(F32) + rank
    put = (slot == iota((SLOTS, ROWS), 0).astype(F32)).astype(BF16)
    loads[1].wait()
    loads[2].wait()
    tail = jnp.concatenate([ckpt[MAIN:VALS, :], rhs[MAIN:VALS, :]], axis=0)
    send[:, 0:256] = dot_t(put, ckpt[0:MAIN, :]).astype(BF16)
    send[:, 256:512] = dot_t(put, rhs[0:MAIN, :]).astype(BF16)
    send[:, 512:640] = dot_t(put, tail).astype(BF16)

    pl.semaphore_wait(barrier, NZ - 1 + ND - 1 + GRP - 1 + 2)

    for p in range(1, NZ):
        rows = pl.ds(p * PIECE, PIECE)
        to = (my_z + ORDER[p]) % NZ * ND + my_d
        remote(send.at[rows], zrecv.at[rows], zs_sem, zr_sem.at[p // PER_CHUNK], blk=to).start()
    zrecv[0:PIECE, :] = send[0:PIECE, :]

    row, col = iota((CHUNK, CHUNK), 0), iota((CHUNK, CHUNK), 1)
    regroup = (col == ((row // CAP) % PER_CHUNK) * PIECE + (row // PART) * CAP + row % CAP).astype(BF16)

    def pass_on(q):
        rows = slice(q * CHUNK, (q + 1) * CHUNK)
        sent = PIECE if q == 0 else 0
        arrived(zrecv.at[pl.ds(q * CHUNK + sent, CHUNK - sent)], zr_sem.at[q])
        moved = dot(regroup, zrecv[rows, :]).astype(BF16)
        zpack[rows, :] = moved
        for e in (4, 5, 3, 2, 6, 7, 1):
            part = pl.ds(q * CHUNK + e * PART, PART)
            to = my_z * ND + (my_d + e) % ND
            remote(zpack.at[part], got.at[part], ds_sem, dr_sem, blk=to).start()
        got[q * CHUNK : q * CHUNK + PART, :] = moved[0:PART, :]

    for load in loads[3:]:
        load.wait()
    table[...] = jnp.zeros_like(table)
    faces = fblk[...]
    side = jnp.where(faces >= 0, ((faces >> 10) - me + 1) & (BLK - 1), -1)
    local = faces & (ROWS - 1)
    packed = ((local >> 7) << 6) + (local & 63)
    away_side = (side >> 1) & 1
    outer = (side == 0) | (side == 2)
    table[0:6, :] = jnp.where(outer, away_side * ROWS + local, -1).astype(F32)
    table[8:14, :] = fw[...]
    table[48:54, :] = jnp.where(side == 1, local, -1).astype(F32)
    table[56:62, :] = jnp.where(outer, away_side * DONORS + packed, -1).astype(F32)
    table[64:70, :] = jnp.where(side == 1, packed, -1).astype(F32)
    table[72:78, :] = ((local >> 6) & 1).astype(F32)
    donors = dblk[...]
    donor_grp = (((donors >> 8) - grp) & (GRP - 1)) - 1
    table[16:18, :] = (donor_grp * DONORS + (donors & (DONORS - 1))).astype(F32)
    table[80:82, :] = (donor_grp * 64 + (donors & 63)).astype(F32)
    table[88:90, :] = ((donors >> 6) & 1).astype(F32)
    table[24:26, :] = dw[...]
    anchor = opos[...] >> 10
    e = (my_d - (anchor & (ND - 1))) & (ND - 1)
    place = place_of(my_z - (anchor >> 3))
    order_row = ((place * ND + e) * ROWS + (opos[...] & (ROWS - 1))).astype(F32)
    base = (place // PER_CHUNK) * CHUNK + e * PART + (place % PER_CHUNK) * CAP
    table[32:33, :] = order_row
    table[40:41, :] = base.astype(F32)
    columns = jnp.transpose(table[...])

    def column(n):
        return columns[:, n : n + 1]

    smaller = (order_row < column(32)).astype(BF16)
    rank = dot(smaller, jnp.ones((ROWS, 128), BF16)).astype(jnp.int32) & (CAP - 1)
    recv_slot = rank.astype(F32) + column(40)
    lanes = iota((ROWS, 128), 1).astype(F32)
    pick = jnp.concatenate(
        [(recv_slot == lanes + 128.0 * t).astype(BF16) for t in range(SLOTS // 128)], axis=1
    )

    def select(ref, first, count):
        lane = iota((ROWS, ref.shape[1]), 1).astype(F32)
        for n in range(count):
            ref[n * ROWS : (n + 1) * ROWS, :] = (column(first + n) == lane).astype(BF16)

    select(halo_hot, 0, 6)
    select(own_hot, 48, 6)
    select(halo_tail_hot, 56, 6)
    select(own_tail_hot, 64, 6)
    select(donor_hot, 16, 2)
    select(donor_tail_hot, 80, 2)

    mats_a[...] = jnp.zeros_like(mats_a)
    mats_b[...] = jnp.zeros_like(mats_b)
    mats_a[0:VALS, 0:VALS] = lmat[...]
    mats_b[0:VALS, 0:VALS] = rmat[...]
    mats_a[:, PADDED:] = jnp.transpose(mats_b[0:PADDED, :])
    mats_b[PADDED:, :] = jnp.transpose(mats_a[:, 0:PADDED])

    for q in range(CHUNKS):
        pass_on(q)
    arrived(got.at[pl.ds(0, SLOTS - SLOTS // ND)], dr_sem)

    half = iota((ROWS, 128), 1) < 64
    last = dot(pick, got[:, 512:640])
    state = jnp.concatenate([dot(pick, got[:, 0:256]), jnp.where(half, last, 0.0)], axis=1)
    diag = 1.0 / (2.0 + state * state)
    inv_diag[...] = diag
    rhs_new = jnp.concatenate(
        [dot(pick, got[:, 256:512]), jnp.where(half, pltpu.roll(last, 64, 1), 0.0)], axis=1
    )
    rhs_f[...] = rhs_new
    value[...] = rhs_new * diag

    def stage(s, h, rows):
        own[s, DONORS * h : DONORS * (h + 1), :] = rows[:, 0:MAIN].astype(BF16)
        low, high = rows[0:64, MAIN:], rows[64:128, MAIN:]
        turned_low, turned_high = pltpu.roll(low, 64, 1), pltpu.roll(high, 64, 1)
        at = slice(64 * h, 64 * h + 64)
        own_tail[s, at, 0:128] = jnp.where(half[0:64], low, turned_high).astype(BF16)
        own_tail[s, at, 128:256] = jnp.where(half[0:64], high, turned_low).astype(BF16)

    def turn(ref, s):
        ref[s, :, 128:256] = pltpu.roll(ref[s, :, 0:128].astype(F32), 64, 1).astype(BF16)

    tail_lanes = pl.ds(0, 128)

    def send_donors(s):
        for g in (2, 1, 3):
            to = (grp + GRP - g) % GRP
            remote(
                own.at[s, pl.ds(0, DONORS)], donor_pool.at[s, pl.ds((g - 1) * DONORS, DONORS)],
                hs_sem.at[s, 2], hr_sem.at[s, 2], grp=to,
            ).start()
            remote(
                own_tail.at[s, pl.ds(0, 64), tail_lanes],
                donor_tail.at[s, pl.ds((g - 1) * 64, 64), tail_lanes],
                hs_sem.at[s, 3], hr_sem.at[s, 3], grp=to,
            ).start()

    def send_halo(s):
        for n, to in enumerate((above, below)):
            remote(
                own.at[s], halo.at[s, pl.ds(n * ROWS, ROWS)],
                hs_sem.at[s, 0], hr_sem.at[s, 0], blk=to,
            ).start()
            remote(
                own_tail.at[s, :, tail_lanes], halo_tail.at[s, pl.ds(n * DONORS, DONORS), tail_lanes],
                hs_sem.at[s, 1], hr_sem.at[s, 1], blk=to,
            ).start()

    def moves(s):
        return (halo.at[s], halo_tail.at[s, :, tail_lanes], donor_pool.at[s], donor_tail.at[s, :, tail_lanes])

    lane = iota((ROWS, 128), 1)

    def face_pass(main_hot, main, tail_hot, tail):
        tiles = [jnp.zeros((ROWS, 128), F32) for _ in range(3)]
        for f in range(6):
            stride = (16, 4, 1)[f // 2]
            cell = lane // stride % 4
            rows = slice(f * ROWS, (f + 1) * ROWS)
            weight = column(8 + f)
            fetched = dot(main_hot[rows, :], main)
            both = dot(tail_hot[rows, :], tail)
            last = jnp.where(column(72 + f) > 0.5, both[:, 128:256], both[:, 0:128])
            for t, part in enumerate((fetched[:, 0:128], fetched[:, 128:256], last)):
                if f % 2 == 0:
                    moved = jnp.where(cell == 0, pltpu.roll(part * weight, 128 - 3 * stride, 1), 0.0)
                else:
                    moved = jnp.where(cell == 3, pltpu.roll(part * weight, 3 * stride, 1), 0.0)
                tiles[t] = tiles[t] + moved
        return jnp.concatenate(tiles, axis=1)

    stage(0, 0, value[0:DONORS, :])
    send_donors(0)
    stage(0, 1, value[DONORS:, :])
    send_halo(0)
    left_gain[...] = 0.5 * jnp.tanh(state)
    right_gain[...] = 0.4 * jnp.tanh(1.5 * state - 0.5)

    for s in range(2):
        rounded = value[...].astype(BF16)
        proj = dot(rounded, mats_a[...])
        mid_l = (proj[:, 0:PADDED] * left_gain[...]).astype(BF16)
        mid_r = (proj[:, PADDED:] * right_gain[...]).astype(BF16)
        applied = dot(mid_l, mats_b[0:PADDED, :]) + dot(mid_r, mats_b[PADDED:, :])
        value[...] = rhs_f[...] - applied
        value[...] = value[...] - face_pass(own_hot, own[s], own_tail_hot, own_tail[s])

        for n in (0, 1):
            arrived(moves(s)[n], hr_sem.at[s, n])
        turn(halo_tail, s)
        value[...] = value[...] - face_pass(halo_hot, halo[s], halo_tail_hot, halo_tail[s])

        for n in (2, 3):
            arrived(moves(s)[n], hr_sem.at[s, n])
        turn(donor_tail, s)
        main = dot(donor_hot[...], donor_pool[s])
        both = dot(donor_tail_hot[...], donor_tail[s])
        fringe = jnp.zeros((ROWS, PADDED), F32)
        for k in range(2):
            rows = slice(k * ROWS, (k + 1) * ROWS)
            last = jnp.where(column(88 + k) > 0.5, both[rows, 128:256], both[rows, 0:128])
            fringe = fringe + jnp.concatenate([main[rows], last], axis=1) * column(24 + k)
        value[...] = (value[...] - fringe) * inv_diag[...]
        if s == 0:
            stage(1, 0, value[0:DONORS, :])
            send_donors(1)
            stage(1, 1, value[DONORS:, :])
            send_halo(1)
    out[...] = jnp.transpose(value[...])[0:VALS, :]
    arrived(send.at[pl.ds(PIECE, SLOTS - PIECE)], zs_sem)
    arrived(zpack.at[pl.ds(0, SLOTS - SLOTS // ND)], ds_sem)
    for s in range(2):
        for n, ref in enumerate(moves(s)):
            arrived(ref, hs_sem.at[s, n])


def body(ckpt, rhs, npos, opos, lmat, rmat, fblk, fw, dblk, dw):
    args = (ckpt.T, rhs.T, npos.reshape(1, ROWS), opos.reshape(1, ROWS), lmat, rmat, fblk, fw, dblk, dw)
    dma = pltpu.SemaphoreType.DMA
    out = pl.pallas_call(
        kernel,
        out_shape=pltpu.VMEM((VALS, ROWS), F32),
        in_specs=[pl.BlockSpec(memory_space=pl.ANY)] * 10,
        out_specs=pl.BlockSpec(memory_space=pltpu.VMEM),
        scratch_shapes=[pltpu.VMEM(a.shape, a.dtype) for a in args]
        + [pltpu.VMEM((SLOTS, PACKED), BF16)] * 4
        + [
            pltpu.VMEM((128, ROWS), F32),
            pltpu.VMEM((6 * ROWS, ROWS), BF16),
            pltpu.VMEM((6 * ROWS, DONORS), BF16),
            pltpu.VMEM((6 * ROWS, 2 * ROWS), BF16),
            pltpu.VMEM((6 * ROWS, 2 * DONORS), BF16),
            pltpu.VMEM((2 * ROWS, 3 * DONORS), BF16),
            pltpu.VMEM((2 * ROWS, 3 * 64), BF16),
            pltpu.VMEM((2, ROWS, MAIN), BF16),
            pltpu.VMEM((2, DONORS, 256), BF16),
            pltpu.VMEM((2, 2 * ROWS, MAIN), BF16),
            pltpu.VMEM((2, 2 * DONORS, 256), BF16),
            pltpu.VMEM((2, 3 * DONORS, MAIN), BF16),
            pltpu.VMEM((2, 3 * 64, 256), BF16),
            pltpu.VMEM((PADDED, 2 * PADDED), BF16),
            pltpu.VMEM((2 * PADDED, PADDED), BF16),
        ]
        + [pltpu.VMEM((ROWS, PADDED), F32)] * 5
        + [dma((len(args),))]
        + [dma(()), dma((CHUNKS,)), dma(()), dma(())]
        + [dma((2, 4))] * 2,
        compiler_params=pltpu.CompilerParams(collective_id=0, has_side_effects=True),
    )(*args)
    return out.T


def solution(mesh):
    row, vec, many = P(("blk", "grp"), None), P(("blk", "grp")), P(None, ("blk", "grp"))
    return jax.shard_map(
        body,
        mesh=mesh,
        in_specs=(row, row, vec, vec, P(), P(), many, many, many, many),
        out_specs=row,
        check_vma=False,
    )
```

time: 67.9 us -> 65.1 us (0.959)
  Pallas kernels: 66.8 us -> 64.2 us
    pallas_call x1, Pallas kernels: 66.8 us -> 64.2 us  [body(): pl.pallas_call(kernel, out_shape=pltpu.VMEM((VALS, ROWS), F32), in_specs=...]
where the time goes in v3:
time: 65.1 us; the launch traced here: 65 us
  Pallas kernels  64.2 us (99%)
  local copies, waits for them, and re-layouts  0.73 us (1%)
    pallas_call x1, Pallas kernels, body(): pl.pallas_call(kernel, out_shape=pltpu.VMEM((VALS, ROWS), F32), in_specs=...  64.2 us

profile of v3, /device:TPU:1, one launch (start us, length us, event | category | flops | bytes accessed | tf_op | source)
XLA Modules:
  0.0 65.0 jit_solution(9539370941712758553)
XLA Ops:
  0.0 64.2 %shard_map.100 = f32[320,256]{1,0:T(8,128)S(1)} custom-call(bf16[320,256]{1,0:T(8,128)(2,1)} %bitcast.6, bf16[320,256]{1,0:T(8,128)(2,1)} %bitcast.7, s32[1,256]{1,0:T(1,128)} %bitcast.8, s32[1,256]{1,0:T(1,128)} %bitcast.9, bf16[320,320]{1,0:T(8,128)(2,1)} %lmat_hbm.1, bf16[320,320]{1,0:T(8,128)(2,1)} %rmat_hbm.1, s32[6,256]{1,0:T(8,128)} %fblk_hbm.1, ...), custom_call_target="tpu_custom_call" | custom-call | tf_op jit(solution)/shard_map/pallas_call | solution.py:315
  64.2 0.7 %copy.12 = f32[256,320]{0,1:T(8,128)} copy(f32[256,320]{0,1:T(8,128)S(1)} %bitcast.5) | data formatting | bytes 655360

commit v4 on v3

v4 whole, which is shorter than its diff:
```python
import jax
import jax.numpy as jnp
from jax import lax
from jax.experimental import pallas as pl
from jax.experimental.pallas import tpu as pltpu
from jax.sharding import PartitionSpec as P

MESH = pl.DeviceIdType.MESH
ROWS = 256
VALS = 320
MAIN = 256
PADDED = 384
BLK = 128
GRP = 4
NZ = 16
ND = 8
CAP = 4
SLOTS = BLK * CAP
DONORS = 128
PIECE = ND * CAP
PART = NZ * CAP
WIDTHS = (256, 256, 128)
F32 = jnp.float32
BF16 = jnp.bfloat16
ORDER = (0, 8, 9, 7, 10, 6, 11, 5, 12, 4, 13, 3, 15, 1, 14, 2)


def dot(a, b):
    return jnp.dot(a, b, preferred_element_type=F32)


def dot_t(a, b):
    return lax.dot_general(a, b, (((1,), (1,)), ((), ())), preferred_element_type=F32)


def iota(shape, dim):
    return lax.broadcasted_iota(jnp.int32, shape, dim)


def place_of(away):
    away = away & (NZ - 1)
    return sum(jnp.where(away == a, p, 0) for p, a in enumerate(ORDER) if p)


def arrived(ref, sem):
    pltpu.make_async_copy(ref, ref, sem).wait()


def remote(src, dst, send_sem, recv_sem, **where):
    return pltpu.make_async_remote_copy(
        src_ref=src, dst_ref=dst, send_sem=send_sem, recv_sem=recv_sem, device_id=where, device_id_type=MESH
    )


def kernel(
    ckpt_hbm, rhs_hbm, npos_hbm, opos_hbm, lmat_hbm, rmat_hbm, fblk_hbm, fw_hbm, dblk_hbm, dw_hbm, out,
    ckpt, rhs, npos, opos, lmat, rmat, fblk, fw, dblk, dw,
    send_0, send_1, send_2, zrecv_0, zrecv_1, zrecv_2, zpack_0, zpack_1, zpack_2, got_0, got_1, got_2, table,
    own_hot, own_tail_hot, halo_hot, halo_tail_hot, donor_hot, donor_tail_hot,
    own, own_tail, halo, halo_tail, donor_pool, donor_tail, mats_a, mats_b,
    left_gain, right_gain, inv_diag, rhs_f, value, rest,
    in_sem, zs_sem, zr_sem, ds_sem, dr_sem, hs_sem, hr_sem,
):
    me = lax.axis_index("blk")
    grp = lax.axis_index("grp")
    my_z, my_d = me // ND, me % ND
    below, above = (me + BLK - 1) % BLK, (me + 1) % BLK

    send, zrecv = (send_0, send_1, send_2), (zrecv_0, zrecv_1, zrecv_2)
    zpack, got = (zpack_0, zpack_1, zpack_2), (got_0, got_1, got_2)

    barrier = pltpu.get_barrier_semaphore()

    def greet(**where):
        pl.semaphore_signal(barrier, inc=1, device_id=where, device_id_type=MESH)

    for away in (8, 7, 9, 6, 10, 5, 11, 4, 12, 3, 13, 2, 14, 1, 15):
        greet(blk=(my_z + away) % NZ * ND + my_d)
    for e in range(1, ND):
        greet(blk=my_z * ND + (my_d + e) % ND)
    for g in range(1, GRP):
        greet(grp=(grp + g) % GRP)
    greet(blk=below)
    greet(blk=above)

    pairs = (
        (npos_hbm, npos), (ckpt_hbm, ckpt), (rhs_hbm, rhs), (opos_hbm, opos), (fblk_hbm, fblk),
        (fw_hbm, fw), (dblk_hbm, dblk), (dw_hbm, dw), (lmat_hbm, lmat), (rmat_hbm, rmat),
    )
    loads = [pltpu.make_async_copy(a, b, in_sem.at[i]) for i, (a, b) in enumerate(pairs)]
    for load in loads:
        load.start()

    loads[0].wait()
    target = npos[...] >> 10
    key = place_of((target >> 3) - my_z) * ND + (((target & (ND - 1)) - my_d) & (ND - 1))
    hot = (key == iota((BLK, ROWS), 0)).astype(BF16)
    earlier = (iota((ROWS, ROWS), 0) < iota((ROWS, ROWS), 1)).astype(BF16)
    rank = jnp.sum(hot.astype(F32) * dot(hot, earlier), axis=0, keepdims=True)
    slot = (key * CAP).astype(F32) + rank
    put = (slot == iota((SLOTS, ROWS), 0).astype(F32)).astype(BF16)
    loads[1].wait()
    loads[2].wait()

    def pack(c):
        last = c == 2
        count = VALS - MAIN if last else 128
        at = slice(128 * c, 128 * c + count)
        both = jnp.concatenate([ckpt[at, :], rhs[at, :]], axis=0)
        send[c][...] = dot_t(put, both).astype(BF16)

    def send_z(c):
        for p in range(1, NZ):
            rows = pl.ds(p * PIECE, PIECE)
            to = (my_z + ORDER[p]) % NZ * ND + my_d
            remote(send[c].at[rows], zrecv[c].at[rows], zs_sem.at[c], zr_sem.at[c], blk=to).start()
        zrecv[c][0:PIECE, :] = send[c][0:PIECE, :]

    pack(0)
    pl.semaphore_wait(barrier, NZ - 1 + ND - 1 + GRP - 1 + 2)
    send_z(0)
    for c in (1, 2):
        pack(c)
        send_z(c)

    row, col = iota((SLOTS, SLOTS), 0), iota((SLOTS, SLOTS), 1)
    regroup = (col == ((row // CAP) % NZ) * PIECE + (row // PART) * CAP + row % CAP).astype(BF16)
    sent_z, sent_d = pl.ds(PIECE, SLOTS - PIECE), pl.ds(PART, SLOTS - PART)

    def pass_on(c):
        arrived(zrecv[c].at[sent_z], zr_sem.at[c])
        moved = dot(regroup, zrecv[c][...]).astype(BF16)
        zpack[c][...] = moved
        for e in (4, 5, 3, 2, 6, 7, 1):
            part = pl.ds(e * PART, PART)
            to = my_z * ND + (my_d + e) % ND
            remote(zpack[c].at[part], got[c].at[part], ds_sem.at[c], dr_sem.at[c], blk=to).start()
        got[c][0:PART, :] = moved[0:PART, :]

    for load in loads[3:]:
        load.wait()
    table[...] = jnp.zeros_like(table)
    faces = fblk[...]
    side = jnp.where(faces >= 0, ((faces >> 10) - me + 1) & (BLK - 1), -1)
    local = faces & (ROWS - 1)
    packed = ((local >> 7) << 6) + (local & 63)
    away_side = (side >> 1) & 1
    outer = (side == 0) | (side == 2)
    table[0:6, :] = jnp.where(outer, away_side * ROWS + local, -1).astype(F32)
    table[8:14, :] = fw[...]
    table[48:54, :] = jnp.where(side == 1, local, -1).astype(F32)
    table[56:62, :] = jnp.where(outer, away_side * DONORS + packed, -1).astype(F32)
    table[64:70, :] = jnp.where(side == 1, packed, -1).astype(F32)
    table[72:78, :] = ((local >> 6) & 1).astype(F32)
    donors = dblk[...]
    donor_grp = (((donors >> 8) - grp) & (GRP - 1)) - 1
    table[16:18, :] = (donor_grp * DONORS + (donors & (DONORS - 1))).astype(F32)
    table[80:82, :] = (donor_grp * 64 + (donors & 63)).astype(F32)
    table[88:90, :] = ((donors >> 6) & 1).astype(F32)
    table[24:26, :] = dw[...]
    anchor = opos[...] >> 10
    e = (my_d - (anchor & (ND - 1))) & (ND - 1)
    place = place_of(my_z - (anchor >> 3))
    order_row = ((place * ND + e) * ROWS + (opos[...] & (ROWS - 1))).astype(F32)
    base = e * PART + place * CAP
    table[32:33, :] = order_row
    table[40:41, :] = base.astype(F32)
    columns = jnp.transpose(table[...])

    def column(n):
        return columns[:, n : n + 1]

    smaller = (order_row < column(32)).astype(BF16)
    rank = dot(smaller, jnp.ones((ROWS, 128), BF16)).astype(jnp.int32) & (CAP - 1)
    recv_slot = rank.astype(F32) + column(40)
    lanes = iota((ROWS, 128), 1).astype(F32)
    pick = jnp.concatenate(
        [(recv_slot == lanes + 128.0 * t).astype(BF16) for t in range(SLOTS // 128)], axis=1
    )

    def select(ref, first, count):
        lane = iota((ROWS, ref.shape[1]), 1).astype(F32)
        for n in range(count):
            ref[n * ROWS : (n + 1) * ROWS, :] = (column(first + n) == lane).astype(BF16)

    select(halo_hot, 0, 6)
    select(own_hot, 48, 6)
    select(halo_tail_hot, 56, 6)
    select(own_tail_hot, 64, 6)
    select(donor_hot, 16, 2)
    select(donor_tail_hot, 80, 2)

    mats_a[...] = jnp.zeros_like(mats_a)
    mats_b[...] = jnp.zeros_like(mats_b)
    mats_a[0:VALS, 0:VALS] = lmat[...]
    mats_b[0:VALS, 0:VALS] = rmat[...]
    mats_a[:, PADDED:] = jnp.transpose(mats_b[0:PADDED, :])
    mats_b[PADDED:, :] = jnp.transpose(mats_a[:, 0:PADDED])

    half = iota((ROWS, 128), 1) < 64

    def unpack(c):
        arrived(got[c].at[sent_d], dr_sem.at[c])
        both = dot(pick, got[c][...])
        if c == 2:
            state = jnp.where(half, both, 0.0)
            right_side = jnp.where(half, pltpu.roll(both, 64, 1), 0.0)
        else:
            state, right_side = both[:, 0:128], both[:, 128:256]
        at = slice(128 * c, 128 * c + 128)
        diag = 1.0 / (2.0 + state * state)
        inv_diag[:, at] = diag
        rhs_f[:, at] = right_side
        value[:, at] = right_side * diag
        return state

    def gains(c, state):
        at = slice(128 * c, 128 * c + 128)
        left_gain[:, at] = 0.5 * jnp.tanh(state)
        right_gain[:, at] = 0.4 * jnp.tanh(1.5 * state - 0.5)

    def stage_tail(s, h, tails):
        low, high = tails[0:64], tails[64:128]
        turned_low, turned_high = pltpu.roll(low, 64, 1), pltpu.roll(high, 64, 1)
        at = slice(64 * h, 64 * h + 64)
        own_tail[s, at, 0:128] = jnp.where(half[0:64], low, turned_high).astype(BF16)
        own_tail[s, at, 128:256] = jnp.where(half[0:64], high, turned_low).astype(BF16)

    def turn(ref, s):
        ref[s, :, 128:256] = pltpu.roll(ref[s, :, 0:128].astype(F32), 64, 1).astype(BF16)

    def lanes_of(t):
        return pl.ds(128 if t == 1 else 0, 128)

    def send_donors(s, t):
        src, dst, rows = (own_tail, donor_tail, 64) if t == 2 else (own, donor_pool, DONORS)
        for g in (2, 1, 3):
            remote(
                src.at[s, pl.ds(0, rows), lanes_of(t)],
                dst.at[s, pl.ds((g - 1) * rows, rows), lanes_of(t)],
                hs_sem.at[s, 3 + t], hr_sem.at[s, 3 + t], grp=(grp + GRP - g) % GRP,
            ).start()

    def send_halo(s, t):
        src, dst, rows = (own_tail, halo_tail, DONORS) if t == 2 else (own, halo, ROWS)
        for n, to in enumerate((above, below)):
            remote(
                src.at[s, :, lanes_of(t)], dst.at[s, pl.ds(n * rows, rows), lanes_of(t)],
                hs_sem.at[s, t], hr_sem.at[s, t], blk=to,
            ).start()

    def moved_bytes(s, n):
        ref = (halo, halo, halo_tail, donor_pool, donor_pool, donor_tail)[n]
        return ref.at[s, :, lanes_of(n % 3)]

    def received(s, n):
        arrived(moved_bytes(s, n), hr_sem.at[s, n])

    lane = iota((ROWS, 128), 1)

    def face_tile(f, part):
        stride = (16, 4, 1)[f // 2]
        cell = lane // stride % 4
        if f % 2 == 0:
            return jnp.where(cell == 0, pltpu.roll(part, 128 - 3 * stride, 1), 0.0)
        return jnp.where(cell == 3, pltpu.roll(part, 3 * stride, 1), 0.0)

    def faces_main(hot, rows_of):
        tiles = [jnp.zeros((ROWS, 128), F32) for _ in range(2)]
        for f in range(6):
            fetched = dot(hot[f * ROWS : (f + 1) * ROWS, :], rows_of) * column(8 + f)
            tiles = [tiles[t] + face_tile(f, fetched[:, 128 * t : 128 * t + 128]) for t in range(2)]
        return jnp.concatenate(tiles, axis=1)

    def faces_tail(hot, rows_of):
        total = jnp.zeros((ROWS, 128), F32)
        for f in range(6):
            both = dot(hot[f * ROWS : (f + 1) * ROWS, :], rows_of)
            picked = jnp.where(column(72 + f) > 0.5, both[:, 128:256], both[:, 0:128])
            total = total + face_tile(f, picked * column(8 + f))
        return total

    def fringe_main(s):
        fetched = dot(donor_hot[...], donor_pool[s])
        return fetched[0:ROWS] * column(24) + fetched[ROWS:] * column(25)

    def fringe_tail(s):
        turn(donor_tail, s)
        both = dot(donor_tail_hot[...], donor_tail[s])
        total = jnp.zeros((ROWS, 128), F32)
        for k in range(2):
            rows = slice(k * ROWS, (k + 1) * ROWS)
            picked = jnp.where(column(88 + k) > 0.5, both[rows, 128:256], both[rows, 0:128])
            total = total + picked * column(24 + k)
        return total

    def applied():
        proj = dot(value[...].astype(BF16), mats_a[...])
        mid_l = (proj[:, 0:PADDED] * left_gain[...]).astype(BF16)
        mid_r = (proj[:, PADDED:] * right_gain[...]).astype(BF16)
        return dot(mid_l, mats_b[0:PADDED, :]) + dot(mid_r, mats_b[PADDED:, :])

    for c in (0, 1):
        pass_on(c)
        state = unpack(c)
        own[0, :, 128 * c : 128 * c + 128] = value[:, 128 * c : 128 * c + 128].astype(BF16)
        send_donors(0, c)
        send_halo(0, c)
        gains(c, state)
    rest[:, 0:MAIN] = rhs_f[:, 0:MAIN] - faces_main(own_hot, own[0])
    pass_on(2)
    received(0, 0)
    received(0, 1)
    rest[:, 0:MAIN] = rest[:, 0:MAIN] - faces_main(halo_hot, halo[0])
    received(0, 3)
    received(0, 4)
    rest[:, 0:MAIN] = rest[:, 0:MAIN] - fringe_main(0)
    state = unpack(2)
    stage_tail(0, 0, value[0:DONORS, MAIN:])
    send_donors(0, 2)
    stage_tail(0, 1, value[DONORS:, MAIN:])
    send_halo(0, 2)
    gains(2, state)
    rest[:, MAIN:] = rhs_f[:, MAIN:] - faces_tail(own_tail_hot, own_tail[0])
    rest[...] = rest[...] - applied()
    received(0, 2)
    turn(halo_tail, 0)
    rest[:, MAIN:] = rest[:, MAIN:] - faces_tail(halo_tail_hot, halo_tail[0])
    received(0, 5)
    rest[:, MAIN:] = rest[:, MAIN:] - fringe_tail(0)
    value[...] = rest[...] * inv_diag[...]

    own[1] = value[:, 0:MAIN].astype(BF16)
    for h in range(2):
        stage_tail(1, h, value[DONORS * h : DONORS * (h + 1), MAIN:])
    for t in range(3):
        send_donors(1, t)
    for t in range(3):
        send_halo(1, t)
    rest[...] = rhs_f[...] - applied()
    rest[:, 0:MAIN] = rest[:, 0:MAIN] - faces_main(own_hot, own[1])
    rest[:, MAIN:] = rest[:, MAIN:] - faces_tail(own_tail_hot, own_tail[1])
    received(1, 0)
    received(1, 1)
    rest[:, 0:MAIN] = rest[:, 0:MAIN] - faces_main(halo_hot, halo[1])
    received(1, 2)
    turn(halo_tail, 1)
    rest[:, MAIN:] = rest[:, MAIN:] - faces_tail(halo_tail_hot, halo_tail[1])
    for n in (3, 4, 5):
        received(1, n)
    rest[:, 0:MAIN] = rest[:, 0:MAIN] - fringe_main(1)
    rest[:, MAIN:] = rest[:, MAIN:] - fringe_tail(1)
    value[...] = rest[...] * inv_diag[...]
    out[...] = jnp.transpose(value[...])[0:VALS, :]
    for c in range(3):
        arrived(send[c].at[sent_z], zs_sem.at[c])
        arrived(zpack[c].at[sent_d], ds_sem.at[c])
    for s in range(2):
        for n in range(6):
            arrived(moved_bytes(s, n), hs_sem.at[s, n])


def body(ckpt, rhs, npos, opos, lmat, rmat, fblk, fw, dblk, dw):
    args = (ckpt.T, rhs.T, npos.reshape(1, ROWS), opos.reshape(1, ROWS), lmat, rmat, fblk, fw, dblk, dw)
    dma = pltpu.SemaphoreType.DMA
    out = pl.pallas_call(
        kernel,
        out_shape=pltpu.VMEM((VALS, ROWS), F32),
        in_specs=[pl.BlockSpec(memory_space=pl.ANY)] * 10,
        out_specs=pl.BlockSpec(memory_space=pltpu.VMEM),
        scratch_shapes=[pltpu.VMEM(a.shape, a.dtype) for a in args]
        + [pltpu.VMEM((SLOTS, width), BF16) for _ in range(4) for width in WIDTHS]
        + [
            pltpu.VMEM((128, ROWS), F32),
            pltpu.VMEM((6 * ROWS, ROWS), BF16),
            pltpu.VMEM((6 * ROWS, DONORS), BF16),
            pltpu.VMEM((6 * ROWS, 2 * ROWS), BF16),
            pltpu.VMEM((6 * ROWS, 2 * DONORS), BF16),
            pltpu.VMEM((2 * ROWS, 3 * DONORS), BF16),
            pltpu.VMEM((2 * ROWS, 3 * 64), BF16),
            pltpu.VMEM((2, ROWS, MAIN), BF16),
            pltpu.VMEM((2, DONORS, 256), BF16),
            pltpu.VMEM((2, 2 * ROWS, MAIN), BF16),
            pltpu.VMEM((2, 2 * DONORS, 256), BF16),
            pltpu.VMEM((2, 3 * DONORS, MAIN), BF16),
            pltpu.VMEM((2, 3 * 64, 256), BF16),
            pltpu.VMEM((PADDED, 2 * PADDED), BF16),
            pltpu.VMEM((2 * PADDED, PADDED), BF16),
        ]
        + [pltpu.VMEM((ROWS, PADDED), F32)] * 6
        + [dma((len(args),))]
        + [dma((3,))] * 4
        + [dma((2, 6))] * 2,
        compiler_params=pltpu.CompilerParams(collective_id=0, has_side_effects=True),
    )(*args)
    return out.T


def solution(mesh):
    row, vec, many = P(("blk", "grp"), None), P(("blk", "grp")), P(None, ("blk", "grp"))
    return jax.shard_map(
        body,
        mesh=mesh,
        in_specs=(row, row, vec, vec, P(), P(), many, many, many, many),
        out_specs=row,
        check_vma=False,
    )
```

time: 65.1 us -> 67.4 us (1.035)
  the two profiles are of different devices: /device:TPU:1 before, /device:TPU:24 now
where the time goes in v4:
time: 67.4 us; the launch traced here: 67.3 us
  Pallas kernels  66.5 us (99%)
  local copies, waits for them, and re-layouts  0.73 us (1%)
    pallas_call x1, Pallas kernels, body(): pl.pallas_call(kernel, out_shape=pltpu.VMEM((VALS, ROWS), F32), in_specs=...  66.5 us

profile of v4, /device:TPU:24, one launch (start us, length us, event | category | flops | bytes accessed | tf_op | source)
XLA Modules:
  0.0 67.3 jit_solution(8929205305996809373)
XLA Ops:
  0.0 66.5 %shard_map.100 = f32[320,256]{1,0:T(8,128)S(1)} custom-call(bf16[320,256]{1,0:T(8,128)(2,1)} %bitcast.6, bf16[320,256]{1,0:T(8,128)(2,1)} %bitcast.7, s32[1,256]{1,0:T(1,128)} %bitcast.8, s32[1,256]{1,0:T(1,128)} %bitcast.9, bf16[320,320]{1,0:T(8,128)(2,1)} %lmat_hbm.1, bf16[320,320]{1,0:T(8,128)(2,1)} %rmat_hbm.1, s32[6,256]{1,0:T(8,128)} %fblk_hbm.1, ...), custom_call_target="tpu_custom_call" | custom-call | tf_op jit(solution)/shard_map/pallas_call | solution.py:366
  66.5 0.7 %copy.12 = f32[256,320]{0,1:T(8,128)} copy(f32[256,320]{0,1:T(8,128)S(1)} %bitcast.5) | data formatting | bytes 655360

commit v5 on v4

--- a/solution.py
+++ b/solution.py
@@ -18,7 +18,8 @@
 SLOTS = BLK * CAP
 DONORS = 128
 PIECE = ND * CAP
-PART = NZ * CAP
+HALF = SLOTS // 2
+PART = HALF // ND
 WIDTHS = (256, 256, 128)
 F32 = jnp.float32
 BF16 = jnp.bfloat16
@@ -55,7 +56,7 @@
 def kernel(
     ckpt_hbm, rhs_hbm, npos_hbm, opos_hbm, lmat_hbm, rmat_hbm, fblk_hbm, fw_hbm, dblk_hbm, dw_hbm, out,
     ckpt, rhs, npos, opos, lmat, rmat, fblk, fw, dblk, dw,
-    send_0, send_1, send_2, zrecv_0, zrecv_1, zrecv_2, zpack_0, zpack_1, zpack_2, got_0, got_1, got_2, table,
+    send_0, send_1, send_2, dgot_0, dgot_1, dgot_2, zpack_0, zpack_1, zpack_2, got_0, got_1, got_2, table,
     own_hot, own_tail_hot, halo_hot, halo_tail_hot, donor_hot, donor_tail_hot,
     own, own_tail, halo, halo_tail, donor_pool, donor_tail, mats_a, mats_b,
     left_gain, right_gain, inv_diag, rhs_f, value, rest,
@@ -66,7 +67,7 @@
     my_z, my_d = me // ND, me % ND
     below, above = (me + BLK - 1) % BLK, (me + 1) % BLK
 
-    send, zrecv = (send_0, send_1, send_2), (zrecv_0, zrecv_1, zrecv_2)
+    send, dgot = (send_0, send_1, send_2), (dgot_0, dgot_1, dgot_2)
     zpack, got = (zpack_0, zpack_1, zpack_2), (got_0, got_1, got_2)
 
     barrier = pltpu.get_barrier_semaphore()
@@ -97,7 +98,8 @@
     hot = (key == iota((BLK, ROWS), 0)).astype(BF16)
     earlier = (iota((ROWS, ROWS), 0) < iota((ROWS, ROWS), 1)).astype(BF16)
     rank = jnp.sum(hot.astype(F32) * dot(hot, earlier), axis=0, keepdims=True)
-    slot = (key * CAP).astype(F32) + rank
+    at = (key >> 6) * HALF + (key & (ND - 1)) * PART + ((key >> 3) & 7) * CAP
+    slot = at.astype(F32) + rank
     put = (slot == iota((SLOTS, ROWS), 0).astype(F32)).astype(BF16)
     loads[1].wait()
     loads[2].wait()
@@ -109,33 +111,40 @@
         both = jnp.concatenate([ckpt[at, :], rhs[at, :]], axis=0)
         send[c][...] = dot_t(put, both).astype(BF16)
 
-    def send_z(c):
-        for p in range(1, NZ):
-            rows = pl.ds(p * PIECE, PIECE)
-            to = (my_z + ORDER[p]) % NZ * ND + my_d
-            remote(send[c].at[rows], zrecv[c].at[rows], zs_sem.at[c], zr_sem.at[c], blk=to).start()
-        zrecv[c][0:PIECE, :] = send[c][0:PIECE, :]
+    def send_d(c):
+        for h in range(2):
+            for e in (4, 5, 3, 2, 6, 7, 1):
+                part = pl.ds(h * HALF + e * PART, PART)
+                to = my_z * ND + (my_d + e) % ND
+                remote(send[c].at[part], dgot[c].at[part], ds_sem.at[c], dr_sem.at[c, h], blk=to).start()
+            kept = slice(h * HALF, h * HALF + PART)
+            dgot[c][kept, :] = send[c][kept, :]
+
+    row, col = iota((HALF, HALF), 0), iota((HALF, HALF), 1)
+    regroup = (col == ((row // CAP) % ND) * PART + (row // PIECE) * CAP + row % CAP).astype(BF16)
+    sent_z, sent_d = pl.ds(PIECE, SLOTS - PIECE), pl.ds(2 * PART, SLOTS - 2 * PART)
+
+    def send_z(c, h):
+        arrived(dgot[c].at[pl.ds(0, HALF - PART)], dr_sem.at[c, h])
+        rows = slice(h * HALF, (h + 1) * HALF)
+        moved = dot(regroup, dgot[c][rows, :]).astype(BF16)
+        zpack[c][rows, :] = moved
+        for p in range(8 * h, 8 * h + 8):
+            if p:
+                part = pl.ds(p * PIECE, PIECE)
+                to = (my_z + ORDER[p]) % NZ * ND + my_d
+                remote(zpack[c].at[part], got[c].at[part], zs_sem.at[c], zr_sem.at[c], blk=to).start()
+        if h == 0:
+            got[c][0:PIECE, :] = moved[0:PIECE, :]
 
     pack(0)
     pl.semaphore_wait(barrier, NZ - 1 + ND - 1 + GRP - 1 + 2)
-    send_z(0)
+    send_d(0)
     for c in (1, 2):
         pack(c)
-        send_z(c)
-
-    row, col = iota((SLOTS, SLOTS), 0), iota((SLOTS, SLOTS), 1)
-    regroup = (col == ((row // CAP) % NZ) * PIECE + (row // PART) * CAP + row % CAP).astype(BF16)
-    sent_z, sent_d = pl.ds(PIECE, SLOTS - PIECE), pl.ds(PART, SLOTS - PART)
-
-    def pass_on(c):
-        arrived(zrecv[c].at[sent_z], zr_sem.at[c])
-        moved = dot(regroup, zrecv[c][...]).astype(BF16)
-        zpack[c][...] = moved
-        for e in (4, 5, 3, 2, 6, 7, 1):
-            part = pl.ds(e * PART, PART)
-            to = my_z * ND + (my_d + e) % ND
-            remote(zpack[c].at[part], got[c].at[part], ds_sem.at[c], dr_sem.at[c], blk=to).start()
-        got[c][0:PART, :] = moved[0:PART, :]
+        send_d(c)
+    send_z(0, 0)
+    send_z(0, 1)
 
     for load in loads[3:]:
         load.wait()
@@ -162,7 +171,7 @@
     e = (my_d - (anchor & (ND - 1))) & (ND - 1)
     place = place_of(my_z - (anchor >> 3))
     order_row = ((place * ND + e) * ROWS + (opos[...] & (ROWS - 1))).astype(F32)
-    base = e * PART + place * CAP
+    base = place * PIECE + e * CAP
     table[32:33, :] = order_row
     table[40:41, :] = base.astype(F32)
     columns = jnp.transpose(table[...])
@@ -200,7 +209,7 @@
     half = iota((ROWS, 128), 1) < 64
 
     def unpack(c):
-        arrived(got[c].at[sent_d], dr_sem.at[c])
+        arrived(got[c].at[sent_z], zr_sem.at[c])
         both = dot(pick, got[c][...])
         if c == 2:
             state = jnp.where(half, both, 0.0)
@@ -300,27 +309,29 @@
         mid_r = (proj[:, PADDED:] * right_gain[...]).astype(BF16)
         return dot(mid_l, mats_b[0:PADDED, :]) + dot(mid_r, mats_b[PADDED:, :])
 
+    for c in (1, 2):
+        send_z(c, 0)
+        send_z(c, 1)
+
     for c in (0, 1):
-        pass_on(c)
         state = unpack(c)
         own[0, :, 128 * c : 128 * c + 128] = value[:, 128 * c : 128 * c + 128].astype(BF16)
         send_donors(0, c)
         send_halo(0, c)
         gains(c, state)
     rest[:, 0:MAIN] = rhs_f[:, 0:MAIN] - faces_main(own_hot, own[0])
-    pass_on(2)
+    state = unpack(2)
+    stage_tail(0, 0, value[0:DONORS, MAIN:])
+    send_donors(0, 2)
+    stage_tail(0, 1, value[DONORS:, MAIN:])
+    send_halo(0, 2)
+    gains(2, state)
     received(0, 0)
     received(0, 1)
     rest[:, 0:MAIN] = rest[:, 0:MAIN] - faces_main(halo_hot, halo[0])
     received(0, 3)
     received(0, 4)
     rest[:, 0:MAIN] = rest[:, 0:MAIN] - fringe_main(0)
-    state = unpack(2)
-    stage_tail(0, 0, value[0:DONORS, MAIN:])
-    send_donors(0, 2)
-    stage_tail(0, 1, value[DONORS:, MAIN:])
-    send_halo(0, 2)
-    gains(2, state)
     rest[:, MAIN:] = rhs_f[:, MAIN:] - faces_tail(own_tail_hot, own_tail[0])
     rest[...] = rest[...] - applied()
     received(0, 2)
@@ -353,8 +364,8 @@
     value[...] = rest[...] * inv_diag[...]
     out[...] = jnp.transpose(value[...])[0:VALS, :]
     for c in range(3):
-        arrived(send[c].at[sent_z], zs_sem.at[c])
-        arrived(zpack[c].at[sent_d], ds_sem.at[c])
+        arrived(send[c].at[sent_d], ds_sem.at[c])
+        arrived(zpack[c].at[sent_z], zs_sem.at[c])
     for s in range(2):
         for n in range(6):
             arrived(moved_bytes(s, n), hs_sem.at[s, n])
@@ -389,7 +400,7 @@
         ]
         + [pltpu.VMEM((ROWS, PADDED), F32)] * 6
         + [dma((len(args),))]
-        + [dma((3,))] * 4
+        + [dma((3,)), dma((3,)), dma((3,)), dma((3, 2))]
         + [dma((2, 6))] * 2,
         compiler_params=pltpu.CompilerParams(collective_id=0, has_side_effects=True),
     )(*args)

time: 67.4 us -> 64.4 us (0.955)
  the two profiles are of different devices: /device:TPU:24 before, /device:TPU:1 now
where the time goes in v5:
time: 64.4 us; the launch traced here: 64.3 us
  Pallas kernels  63.6 us (99%)
  local copies, waits for them, and re-layouts  0.73 us (1%)
    pallas_call x1, Pallas kernels, body(): pl.pallas_call(kernel, out_shape=pltpu.VMEM((VALS, ROWS), F32), in_specs=...  63.6 us

profile of v5, /device:TPU:1, one launch (start us, length us, event | category | flops | bytes accessed | tf_op | source)
XLA Modules:
  0.0 64.3 jit_solution(10911980485825910116)
XLA Ops:
  0.0 63.6 %shard_map.100 = f32[320,256]{1,0:T(8,128)S(1)} custom-call(bf16[320,256]{1,0:T(8,128)(2,1)} %bitcast.6, bf16[320,256]{1,0:T(8,128)(2,1)} %bitcast.7, s32[1,256]{1,0:T(1,128)} %bitcast.8, s32[1,256]{1,0:T(1,128)} %bitcast.9, bf16[320,320]{1,0:T(8,128)(2,1)} %lmat_hbm.1, bf16[320,320]{1,0:T(8,128)(2,1)} %rmat_hbm.1, s32[6,256]{1,0:T(8,128)} %fblk_hbm.1, ...), custom_call_target="tpu_custom_call" | custom-call | tf_op jit(solution)/shard_map/pallas_call | solution.py:377
  63.6 0.7 %copy.12 = f32[256,320]{0,1:T(8,128)} copy(f32[256,320]{0,1:T(8,128)S(1)} %bitcast.5) | data formatting | bytes 655360

commit v6 on v5

--- a/solution.py
+++ b/solution.py
@@ -56,11 +56,11 @@
 def kernel(
     ckpt_hbm, rhs_hbm, npos_hbm, opos_hbm, lmat_hbm, rmat_hbm, fblk_hbm, fw_hbm, dblk_hbm, dw_hbm, out,
     ckpt, rhs, npos, opos, lmat, rmat, fblk, fw, dblk, dw,
-    send_0, send_1, send_2, dgot_0, dgot_1, dgot_2, zpack_0, zpack_1, zpack_2, got_0, got_1, got_2, table,
+    send_0, send_1, send_2, dgot_0, dgot_1, dgot_2, zpack_0, zpack_1, zpack_2, got_0, got_1, got_2, mid, mid_pack, table,
     own_hot, own_tail_hot, halo_hot, halo_tail_hot, donor_hot, donor_tail_hot,
     own, own_tail, halo, halo_tail, donor_pool, donor_tail, mats_a, mats_b,
     left_gain, right_gain, inv_diag, rhs_f, value, rest,
-    in_sem, zs_sem, zr_sem, ds_sem, dr_sem, hs_sem, hr_sem,
+    in_sem, zs_sem, zr_sem, ds_sem, dr_sem, mid_sem, hs_sem, hr_sem,
 ):
     me = lax.axis_index("blk")
     grp = lax.axis_index("grp")
@@ -99,8 +99,10 @@
     earlier = (iota((ROWS, ROWS), 0) < iota((ROWS, ROWS), 1)).astype(BF16)
     rank = jnp.sum(hot.astype(F32) * dot(hot, earlier), axis=0, keepdims=True)
     at = (key >> 6) * HALF + (key & (ND - 1)) * PART + ((key >> 3) & 7) * CAP
-    slot = at.astype(F32) + rank
-    put = (slot == iota((SLOTS, ROWS), 0).astype(F32)).astype(BF16)
+    slots = iota((SLOTS, ROWS), 0).astype(F32)
+    put = (at.astype(F32) + rank == slots).astype(BF16)
+    at = jnp.where(key < BLK // 2, key * CAP, at)
+    put_first = (at.astype(F32) + rank == slots).astype(BF16)
     loads[1].wait()
     loads[2].wait()
 
@@ -109,10 +111,10 @@
         count = VALS - MAIN if last else 128
         at = slice(128 * c, 128 * c + count)
         both = jnp.concatenate([ckpt[at, :], rhs[at, :]], axis=0)
-        send[c][...] = dot_t(put, both).astype(BF16)
+        send[c][...] = dot_t(put if c else put_first, both).astype(BF16)
 
     def send_d(c):
-        for h in range(2):
+        for h in range(2) if c else (1,):
             for e in (4, 5, 3, 2, 6, 7, 1):
                 part = pl.ds(h * HALF + e * PART, PART)
                 to = my_z * ND + (my_d + e) % ND
@@ -137,14 +139,33 @@
         if h == 0:
             got[c][0:PIECE, :] = moved[0:PIECE, :]
 
+    half_rows, half_sent = pl.ds(HALF, HALF), pl.ds(PIECE, HALF - PIECE)
+
+    def first_z():
+        for p in range(1, 8):
+            part = pl.ds(p * PIECE, PIECE)
+            to = (my_z + ORDER[p]) % NZ * ND + my_d
+            remote(send[0].at[part], mid.at[part], mid_sem.at[0], mid_sem.at[1], blk=to).start()
+        mid[0:PIECE, :] = send[0][0:PIECE, :]
+
+    def first_d():
+        arrived(mid.at[half_sent], mid_sem.at[1])
+        back = (col == ((row // CAP) % ND) * PIECE + (row // PART) * CAP + row % CAP).astype(BF16)
+        moved = dot(back, mid[...]).astype(BF16)
+        mid_pack[...] = moved
+        for e in (4, 5, 3, 2, 6, 7, 1):
+            part = pl.ds(e * PART, PART)
+            to = my_z * ND + (my_d + e) % ND
+            remote(mid_pack.at[part], got[0].at[part], mid_sem.at[2], mid_sem.at[3], blk=to).start()
+        got[0][0:PART, :] = moved[0:PART, :]
+
     pack(0)
     pl.semaphore_wait(barrier, NZ - 1 + ND - 1 + GRP - 1 + 2)
+    first_z()
     send_d(0)
     for c in (1, 2):
         pack(c)
         send_d(c)
-    send_z(0, 0)
-    send_z(0, 1)
 
     for load in loads[3:]:
         load.wait()
@@ -174,6 +195,7 @@
     base = place * PIECE + e * CAP
     table[32:33, :] = order_row
     table[40:41, :] = base.astype(F32)
+    table[41:42, :] = jnp.where(place < ND, e * PART + place * CAP, base).astype(F32)
     columns = jnp.transpose(table[...])
 
     def column(n):
@@ -181,11 +203,15 @@
 
     smaller = (order_row < column(32)).astype(BF16)
     rank = dot(smaller, jnp.ones((ROWS, 128), BF16)).astype(jnp.int32) & (CAP - 1)
-    recv_slot = rank.astype(F32) + column(40)
     lanes = iota((ROWS, 128), 1).astype(F32)
-    pick = jnp.concatenate(
-        [(recv_slot == lanes + 128.0 * t).astype(BF16) for t in range(SLOTS // 128)], axis=1
-    )
+
+    def picks(n):
+        recv_slot = rank.astype(F32) + column(n)
+        return jnp.concatenate(
+            [(recv_slot == lanes + 128.0 * t).astype(BF16) for t in range(SLOTS // 128)], axis=1
+        )
+
+    pick, pick_first = picks(40), picks(41)
 
     def select(ref, first, count):
         lane = iota((ROWS, ref.shape[1]), 1).astype(F32)
@@ -209,8 +235,10 @@
     half = iota((ROWS, 128), 1) < 64
 
     def unpack(c):
-        arrived(got[c].at[sent_z], zr_sem.at[c])
-        both = dot(pick, got[c][...])
+        arrived(got[c].at[sent_z if c else half_rows], zr_sem.at[c])
+        if c == 0:
+            arrived(got[0].at[pl.ds(PART, HALF - PART)], mid_sem.at[3])
+        both = dot(pick if c else pick_first, got[c][...])
         if c == 2:
             state = jnp.where(half, both, 0.0)
             right_side = jnp.where(half, pltpu.roll(both, 64, 1), 0.0)
@@ -309,9 +337,11 @@
         mid_r = (proj[:, PADDED:] * right_gain[...]).astype(BF16)
         return dot(mid_l, mats_b[0:PADDED, :]) + dot(mid_r, mats_b[PADDED:, :])
 
+    send_z(0, 1)
     for c in (1, 2):
         send_z(c, 0)
         send_z(c, 1)
+    first_d()
 
     for c in (0, 1):
         state = unpack(c)
@@ -364,8 +394,10 @@
     value[...] = rest[...] * inv_diag[...]
     out[...] = jnp.transpose(value[...])[0:VALS, :]
     for c in range(3):
-        arrived(send[c].at[sent_d], ds_sem.at[c])
-        arrived(zpack[c].at[sent_z], zs_sem.at[c])
+        arrived(send[c].at[sent_d if c else pl.ds(0, HALF - PART)], ds_sem.at[c])
+        arrived(zpack[c].at[sent_z if c else half_rows], zs_sem.at[c])
+    arrived(mid.at[half_sent], mid_sem.at[0])
+    arrived(mid_pack.at[pl.ds(PART, HALF - PART)], mid_sem.at[2])
     for s in range(2):
         for n in range(6):
             arrived(moved_bytes(s, n), hs_sem.at[s, n])
@@ -381,6 +413,7 @@
         out_specs=pl.BlockSpec(memory_space=pltpu.VMEM),
         scratch_shapes=[pltpu.VMEM(a.shape, a.dtype) for a in args]
         + [pltpu.VMEM((SLOTS, width), BF16) for _ in range(4) for width in WIDTHS]
+        + [pltpu.VMEM((HALF, WIDTHS[0]), BF16)] * 2
         + [
             pltpu.VMEM((128, ROWS), F32),
             pltpu.VMEM((6 * ROWS, ROWS), BF16),
@@ -400,7 +433,7 @@
         ]
         + [pltpu.VMEM((ROWS, PADDED), F32)] * 6
         + [dma((len(args),))]
-        + [dma((3,)), dma((3,)), dma((3,)), dma((3, 2))]
+        + [dma((3,)), dma((3,)), dma((3,)), dma((3, 2)), dma((4,))]
         + [dma((2, 6))] * 2,
         compiler_params=pltpu.CompilerParams(collective_id=0, has_side_effects=True),
     )(*args)

time: 64.4 us -> 58.9 us (0.915)
  Pallas kernels: 63.6 us -> 58 us
    pallas_call x1, Pallas kernels: 63.6 us -> 58 us  [body(): pl.pallas_call(kernel, out_shape=pltpu.VMEM((VALS, ROWS), F32), in_specs=...]
where the time goes in v6:
time: 58.9 us; the launch traced here: 58.8 us
  Pallas kernels  58 us (98%)
  local copies, waits for them, and re-layouts  0.73 us (1%)
    pallas_call x1, Pallas kernels, body(): pl.pallas_call(kernel, out_shape=pltpu.VMEM((VALS, ROWS), F32), in_specs=...  58 us

profile of v6, /device:TPU:1, one launch (start us, length us, event | category | flops | bytes accessed | tf_op | source)
XLA Modules:
  0.0 58.8 jit_solution(16596320238112938298)
XLA Ops:
  0.0 58.0 %shard_map.100 = f32[320,256]{1,0:T(8,128)S(1)} custom-call(bf16[320,256]{1,0:T(8,128)(2,1)} %bitcast.6, bf16[320,256]{1,0:T(8,128)(2,1)} %bitcast.7, s32[1,256]{1,0:T(1,128)} %bitcast.8, s32[1,256]{1,0:T(1,128)} %bitcast.9, bf16[320,320]{1,0:T(8,128)(2,1)} %lmat_hbm.1, bf16[320,320]{1,0:T(8,128)(2,1)} %rmat_hbm.1, s32[6,256]{1,0:T(8,128)} %fblk_hbm.1, ...), custom_call_target="tpu_custom_call" | custom-call | tf_op jit(solution)/shard_map/pallas_call | solution.py:409
  58.1 0.7 %copy.12 = f32[256,320]{0,1:T(8,128)} copy(f32[256,320]{0,1:T(8,128)S(1)} %bitcast.5) | data formatting | bytes 655360

commit v7 on v6

--- a/solution.py
+++ b/solution.py
@@ -59,6 +59,7 @@
     send_0, send_1, send_2, dgot_0, dgot_1, dgot_2, zpack_0, zpack_1, zpack_2, got_0, got_1, got_2, mid, mid_pack, table,
     own_hot, own_tail_hot, halo_hot, halo_tail_hot, donor_hot, donor_tail_hot,
     own, own_tail, halo, halo_tail, donor_pool, donor_tail, mats_a, mats_b,
+    face_scale, low_scale, high_scale, donor_scale, donor_low, donor_high,
     left_gain, right_gain, inv_diag, rhs_f, value, rest,
     in_sem, zs_sem, zr_sem, ds_sem, dr_sem, mid_sem, hs_sem, hr_sem,
 ):
@@ -225,6 +226,21 @@
     select(donor_hot, 16, 2)
     select(donor_tail_hot, 80, 2)
 
+    lane = iota((ROWS, 128), 1)
+    for f in range(6):
+        cell = lane // (16, 4, 1)[f // 2] % 4
+        scale = jnp.where(cell == (3 if f % 2 == 0 else 0), column(8 + f), 0.0)
+        face_scale[f] = scale
+        high = jnp.broadcast_to(column(72 + f), (ROWS, 128))
+        low_scale[f] = jnp.where(high > 0.5, 0.0, scale)
+        high_scale[f] = jnp.where(high > 0.5, scale, 0.0)
+    for k in range(2):
+        scale = jnp.broadcast_to(column(24 + k), (ROWS, 128))
+        donor_scale[k] = scale
+        high = jnp.broadcast_to(column(88 + k), (ROWS, 128))
+        donor_low[k] = jnp.where(high > 0.5, 0.0, scale)
+        donor_high[k] = jnp.where(high > 0.5, scale, 0.0)
+
     mats_a[...] = jnp.zeros_like(mats_a)
     mats_b[...] = jnp.zeros_like(mats_b)
     mats_a[0:VALS, 0:VALS] = lmat[...]
@@ -293,42 +309,39 @@
     def received(s, n):
         arrived(moved_bytes(s, n), hr_sem.at[s, n])
 
-    lane = iota((ROWS, 128), 1)
-
-    def face_tile(f, part):
+    def placed(f, part):
         stride = (16, 4, 1)[f // 2]
-        cell = lane // stride % 4
-        if f % 2 == 0:
-            return jnp.where(cell == 0, pltpu.roll(part, 128 - 3 * stride, 1), 0.0)
-        return jnp.where(cell == 3, pltpu.roll(part, 3 * stride, 1), 0.0)
+        return pltpu.roll(part, 128 - 3 * stride if f % 2 == 0 else 3 * stride, 1)
 
     def faces_main(hot, rows_of):
         tiles = [jnp.zeros((ROWS, 128), F32) for _ in range(2)]
         for f in range(6):
-            fetched = dot(hot[f * ROWS : (f + 1) * ROWS, :], rows_of) * column(8 + f)
-            tiles = [tiles[t] + face_tile(f, fetched[:, 128 * t : 128 * t + 128]) for t in range(2)]
+            fetched = dot(hot[f * ROWS : (f + 1) * ROWS, :], rows_of)
+            scale = face_scale[f]
+            tiles = [tiles[t] + placed(f, fetched[:, 128 * t : 128 * t + 128] * scale) for t in range(2)]
         return jnp.concatenate(tiles, axis=1)
 
     def faces_tail(hot, rows_of):
         total = jnp.zeros((ROWS, 128), F32)
         for f in range(6):
             both = dot(hot[f * ROWS : (f + 1) * ROWS, :], rows_of)
-            picked = jnp.where(column(72 + f) > 0.5, both[:, 128:256], both[:, 0:128])
-            total = total + face_tile(f, picked * column(8 + f))
+            total = total + placed(f, both[:, 0:128] * low_scale[f] + both[:, 128:256] * high_scale[f])
         return total
 
     def fringe_main(s):
-        fetched = dot(donor_hot[...], donor_pool[s])
-        return fetched[0:ROWS] * column(24) + fetched[ROWS:] * column(25)
+        total = [jnp.zeros((ROWS, 128), F32) for _ in range(2)]
+        for k in range(2):
+            fetched = dot(donor_hot[k * ROWS : (k + 1) * ROWS, :], donor_pool[s])
+            scale = donor_scale[k]
+            total = [total[t] + fetched[:, 128 * t : 128 * t + 128] * scale for t in range(2)]
+        return jnp.concatenate(total, axis=1)
 
     def fringe_tail(s):
         turn(donor_tail, s)
-        both = dot(donor_tail_hot[...], donor_tail[s])
         total = jnp.zeros((ROWS, 128), F32)
         for k in range(2):
-            rows = slice(k * ROWS, (k + 1) * ROWS)
-            picked = jnp.where(column(88 + k) > 0.5, both[rows, 128:256], both[rows, 0:128])
-            total = total + picked * column(24 + k)
+            both = dot(donor_tail_hot[k * ROWS : (k + 1) * ROWS, :], donor_tail[s])
+            total = total + both[:, 0:128] * donor_low[k] + both[:, 128:256] * donor_high[k]
         return total
 
     def applied():
@@ -364,35 +377,38 @@
     rest[:, 0:MAIN] = rest[:, 0:MAIN] - fringe_main(0)
     rest[:, MAIN:] = rhs_f[:, MAIN:] - faces_tail(own_tail_hot, own_tail[0])
     rest[...] = rest[...] - applied()
+    value[:, 0:MAIN] = rest[:, 0:MAIN] * inv_diag[:, 0:MAIN]
+    own[1] = value[:, 0:MAIN].astype(BF16)
+    for t in (0, 1):
+        send_donors(1, t)
+    for t in (0, 1):
+        send_halo(1, t)
+    rest[:, 0:MAIN] = rhs_f[:, 0:MAIN] - faces_main(own_hot, own[1])
     received(0, 2)
     turn(halo_tail, 0)
     rest[:, MAIN:] = rest[:, MAIN:] - faces_tail(halo_tail_hot, halo_tail[0])
     received(0, 5)
-    rest[:, MAIN:] = rest[:, MAIN:] - fringe_tail(0)
-    value[...] = rest[...] * inv_diag[...]
-
-    own[1] = value[:, 0:MAIN].astype(BF16)
-    for h in range(2):
-        stage_tail(1, h, value[DONORS * h : DONORS * (h + 1), MAIN:])
-    for t in range(3):
-        send_donors(1, t)
-    for t in range(3):
-        send_halo(1, t)
-    rest[...] = rhs_f[...] - applied()
-    rest[:, 0:MAIN] = rest[:, 0:MAIN] - faces_main(own_hot, own[1])
-    rest[:, MAIN:] = rest[:, MAIN:] - faces_tail(own_tail_hot, own_tail[1])
+    value[:, MAIN:] = (rest[:, MAIN:] - fringe_tail(0)) * inv_diag[:, MAIN:]
+
+    stage_tail(1, 0, value[0:DONORS, MAIN:])
+    send_donors(1, 2)
+    stage_tail(1, 1, value[DONORS:, MAIN:])
+    send_halo(1, 2)
+    rest[:, MAIN:] = rhs_f[:, MAIN:] - faces_tail(own_tail_hot, own_tail[1])
+    rest[...] = rest[...] - applied()
     received(1, 0)
     received(1, 1)
     rest[:, 0:MAIN] = rest[:, 0:MAIN] - faces_main(halo_hot, halo[1])
+    received(1, 3)
+    received(1, 4)
+    rest[:, 0:MAIN] = rest[:, 0:MAIN] - fringe_main(1)
+    out[0:MAIN, :] = jnp.transpose(rest[:, 0:MAIN] * inv_diag[:, 0:MAIN])
     received(1, 2)
     turn(halo_tail, 1)
     rest[:, MAIN:] = rest[:, MAIN:] - faces_tail(halo_tail_hot, halo_tail[1])
-    for n in (3, 4, 5):
-        received(1, n)
-    rest[:, 0:MAIN] = rest[:, 0:MAIN] - fringe_main(1)
-    rest[:, MAIN:] = rest[:, MAIN:] - fringe_tail(1)
-    value[...] = rest[...] * inv_diag[...]
-    out[...] = jnp.transpose(value[...])[0:VALS, :]
+    received(1, 5)
+    last = (rest[:, MAIN:] - fringe_tail(1)) * inv_diag[:, MAIN:]
+    out[MAIN:VALS, :] = jnp.transpose(last)[0 : VALS - MAIN, :]
     for c in range(3):
         arrived(send[c].at[sent_d if c else pl.ds(0, HALF - PART)], ds_sem.at[c])
         arrived(zpack[c].at[sent_z if c else half_rows], zs_sem.at[c])
@@ -431,6 +447,8 @@
             pltpu.VMEM((PADDED, 2 * PADDED), BF16),
             pltpu.VMEM((2 * PADDED, PADDED), BF16),
         ]
+        + [pltpu.VMEM((6, ROWS, 128), F32)] * 3
+        + [pltpu.VMEM((2, ROWS, 128), F32)] * 3
         + [pltpu.VMEM((ROWS, PADDED), F32)] * 6
         + [dma((len(args),))]
         + [dma((3,)), dma((3,)), dma((3,)), dma((3, 2)), dma((4,))]

time: 58.9 us -> 57.3 us (0.973)
  Pallas kernels: 58 us -> 56 us
    pallas_call x1, Pallas kernels: 58 us -> 56 us  [body(): pl.pallas_call(kernel, out_shape=pltpu.VMEM((VALS, ROWS), F32), in_specs=...]
where the time goes in v7:
time: 57.3 us; the launch traced here: 56.7 us
  Pallas kernels  56 us (98%)
  local copies, waits for them, and re-layouts  0.73 us (1%)
    pallas_call x1, Pallas kernels, body(): pl.pallas_call(kernel, out_shape=pltpu.VMEM((VALS, ROWS), F32), in_specs=...  56 us

profile of v7, /device:TPU:1, one launch (start us, length us, event | category | flops | bytes accessed | tf_op | source)
XLA Modules:
  0.0 56.7 jit_solution(712314945866541)
XLA Ops:
  0.0 56.0 %shard_map.100 = f32[320,256]{1,0:T(8,128)S(1)} custom-call(bf16[320,256]{1,0:T(8,128)(2,1)} %bitcast.6, bf16[320,256]{1,0:T(8,128)(2,1)} %bitcast.7, s32[1,256]{1,0:T(1,128)} %bitcast.8, s32[1,256]{1,0:T(1,128)} %bitcast.9, bf16[320,320]{1,0:T(8,128)(2,1)} %lmat_hbm.1, bf16[320,320]{1,0:T(8,128)(2,1)} %rmat_hbm.1, s32[6,256]{1,0:T(8,128)} %fblk_hbm.1, ...), custom_call_target="tpu_custom_call" | custom-call | tf_op jit(solution)/shard_map/pallas_call | solution.py:425
  56.0 0.7 %copy.12 = f32[256,320]{0,1:T(8,128)} copy(f32[256,320]{0,1:T(8,128)S(1)} %bitcast.5) | data formatting | bytes 655360

commit v8 on v7

--- a/solution.py
+++ b/solution.py
@@ -369,21 +369,20 @@
     stage_tail(0, 1, value[DONORS:, MAIN:])
     send_halo(0, 2)
     gains(2, state)
+    rest[:, MAIN:] = rhs_f[:, MAIN:] - faces_tail(own_tail_hot, own_tail[0])
+    rest[...] = rest[...] - applied()
     received(0, 0)
     received(0, 1)
     rest[:, 0:MAIN] = rest[:, 0:MAIN] - faces_main(halo_hot, halo[0])
     received(0, 3)
     received(0, 4)
     rest[:, 0:MAIN] = rest[:, 0:MAIN] - fringe_main(0)
-    rest[:, MAIN:] = rhs_f[:, MAIN:] - faces_tail(own_tail_hot, own_tail[0])
-    rest[...] = rest[...] - applied()
     value[:, 0:MAIN] = rest[:, 0:MAIN] * inv_diag[:, 0:MAIN]
     own[1] = value[:, 0:MAIN].astype(BF16)
     for t in (0, 1):
         send_donors(1, t)
     for t in (0, 1):
         send_halo(1, t)
-    rest[:, 0:MAIN] = rhs_f[:, 0:MAIN] - faces_main(own_hot, own[1])
     received(0, 2)
     turn(halo_tail, 0)
     rest[:, MAIN:] = rest[:, MAIN:] - faces_tail(halo_tail_hot, halo_tail[0])
@@ -394,18 +393,19 @@
     send_donors(1, 2)
     stage_tail(1, 1, value[DONORS:, MAIN:])
     send_halo(1, 2)
+    rest[:, 0:MAIN] = rhs_f[:, 0:MAIN] - faces_main(own_hot, own[1])
     rest[:, MAIN:] = rhs_f[:, MAIN:] - faces_tail(own_tail_hot, own_tail[1])
     rest[...] = rest[...] - applied()
     received(1, 0)
     received(1, 1)
     rest[:, 0:MAIN] = rest[:, 0:MAIN] - faces_main(halo_hot, halo[1])
+    received(1, 2)
+    turn(halo_tail, 1)
+    rest[:, MAIN:] = rest[:, MAIN:] - faces_tail(halo_tail_hot, halo_tail[1])
     received(1, 3)
     received(1, 4)
     rest[:, 0:MAIN] = rest[:, 0:MAIN] - fringe_main(1)
     out[0:MAIN, :] = jnp.transpose(rest[:, 0:MAIN] * inv_diag[:, 0:MAIN])
-    received(1, 2)
-    turn(halo_tail, 1)
-    rest[:, MAIN:] = rest[:, MAIN:] - faces_tail(halo_tail_hot, halo_tail[1])
     received(1, 5)
     last = (rest[:, MAIN:] - fringe_tail(1)) * inv_diag[:, MAIN:]
     out[MAIN:VALS, :] = jnp.transpose(last)[0 : VALS - MAIN, :]

time: 57.3 us -> 57.2 us (level)
  no operation moved by 1% of the time
where the time goes in v8:
time: 57.2 us; the launch traced here: 57.1 us
  Pallas kernels  56.3 us (98%)
  local copies, waits for them, and re-layouts  0.73 us (1%)
    pallas_call x1, Pallas kernels, body(): pl.pallas_call(kernel, out_shape=pltpu.VMEM((VALS, ROWS), F32), in_specs=...  56.3 us

profile of v8, /device:TPU:1, one launch (start us, length us, event | category | flops | bytes accessed | tf_op | source)
XLA Modules:
  0.0 57.1 jit_solution(12058043510881642340)
XLA Ops:
  0.0 56.3 %shard_map.100 = f32[320,256]{1,0:T(8,128)S(1)} custom-call(bf16[320,256]{1,0:T(8,128)(2,1)} %bitcast.6, bf16[320,256]{1,0:T(8,128)(2,1)} %bitcast.7, s32[1,256]{1,0:T(1,128)} %bitcast.8, s32[1,256]{1,0:T(1,128)} %bitcast.9, bf16[320,320]{1,0:T(8,128)(2,1)} %lmat_hbm.1, bf16[320,320]{1,0:T(8,128)(2,1)} %rmat_hbm.1, s32[6,256]{1,0:T(8,128)} %fblk_hbm.1, ...), custom_call_target="tpu_custom_call" | custom-call | tf_op jit(solution)/shard_map/pallas_call | solution.py:425
  56.3 0.7 %copy.12 = f32[256,320]{0,1:T(8,128)} copy(f32[256,320]{0,1:T(8,128)S(1)} %bitcast.5) | data formatting | bytes 655360

commit v9 on v8

--- a/solution.py
+++ b/solution.py
@@ -76,6 +76,14 @@
     def greet(**where):
         pl.semaphore_signal(barrier, inc=1, device_id=where, device_id_type=MESH)
 
+    pairs = (
+        (npos_hbm, npos), (ckpt_hbm, ckpt), (rhs_hbm, rhs), (opos_hbm, opos), (fblk_hbm, fblk),
+        (fw_hbm, fw), (dblk_hbm, dblk), (dw_hbm, dw), (lmat_hbm, lmat), (rmat_hbm, rmat),
+    )
+    loads = [pltpu.make_async_copy(a, b, in_sem.at[i]) for i, (a, b) in enumerate(pairs)]
+    for load in loads:
+        load.start()
+
     for away in (8, 7, 9, 6, 10, 5, 11, 4, 12, 3, 13, 2, 14, 1, 15):
         greet(blk=(my_z + away) % NZ * ND + my_d)
     for e in range(1, ND):
@@ -84,14 +92,6 @@
         greet(grp=(grp + g) % GRP)
     greet(blk=below)
     greet(blk=above)
-
-    pairs = (
-        (npos_hbm, npos), (ckpt_hbm, ckpt), (rhs_hbm, rhs), (opos_hbm, opos), (fblk_hbm, fblk),
-        (fw_hbm, fw), (dblk_hbm, dblk), (dw_hbm, dw), (lmat_hbm, lmat), (rmat_hbm, rmat),
-    )
-    loads = [pltpu.make_async_copy(a, b, in_sem.at[i]) for i, (a, b) in enumerate(pairs)]
-    for load in loads:
-        load.start()
 
     loads[0].wait()
     target = npos[...] >> 10

time: 57.2 us -> 57.2 us (level)
  no operation moved by 1% of the time
where the time goes in v9:
time: 57.2 us; the launch traced here: 57.1 us
  Pallas kernels  56.3 us (98%)
  local copies, waits for them, and re-layouts  0.73 us (1%)
    pallas_call x1, Pallas kernels, body(): pl.pallas_call(kernel, out_shape=pltpu.VMEM((VALS, ROWS), F32), in_specs=...  56.3 us

profile of v9, /device:TPU:1, one launch (start us, length us, event | category | flops | bytes accessed | tf_op | source)
XLA Modules:
  0.0 57.1 jit_solution(3789570585998766131)
XLA Ops:
  0.0 56.3 %shard_map.100 = f32[320,256]{1,0:T(8,128)S(1)} custom-call(bf16[320,256]{1,0:T(8,128)(2,1)} %bitcast.6, bf16[320,256]{1,0:T(8,128)(2,1)} %bitcast.7, s32[1,256]{1,0:T(1,128)} %bitcast.8, s32[1,256]{1,0:T(1,128)} %bitcast.9, bf16[320,320]{1,0:T(8,128)(2,1)} %lmat_hbm.1, bf16[320,320]{1,0:T(8,128)(2,1)} %rmat_hbm.1, s32[6,256]{1,0:T(8,128)} %fblk_hbm.1, ...), custom_call_target="tpu_custom_call" | custom-call | tf_op jit(solution)/shard_map/pallas_call | solution.py:425
  56.4 0.7 %copy.12 = f32[256,320]{0,1:T(8,128)} copy(f32[256,320]{0,1:T(8,128)S(1)} %bitcast.5) | data formatting | bytes 655360
